TPU v7x, 512 devices: a whole 4x4x16 slice. The times are simulated.
512 devices in a mesh: grp: 16 (over y, x), ctx: 32 (over z, core).
Axes of the slice: x: 4, y: 4, z: 16, core: 2. Of those that a mesh axis runs over, the one named last changes fastest.
Arguments:
- queries: bfloat16 [262144, 1024], P(('grp', 'ctx')), may hold values from -6 to 6
- keys: bfloat16 [262144, 1024], P(('grp', 'ctx')), may hold values from -6 to 6
- values: bfloat16 [262144, 1024], P(('grp', 'ctx')), may hold values from -6 to 6
- level_weights: float32 [13, 8, 262144], P(None, None, ('grp', 'ctx')), may hold values from 0.1 to 1.5
Outputs:
- attended: bfloat16 [262144, 1024], P(('grp', 'ctx'))
All inputs are finite; a program needn't handle non-finite values.
Results may differ from a plain program's by a relative error of at most 0.0095.
Values may be sent and summed in bfloat16 or wider, within the bound.
No kernel may reach another device: no remote copies, remote signals or barrier semaphores. Data moves between devices by JAX's collectives and lax.ppermute only.
A program may use at most 64 MiB of HBM per device.

v0:
```python
import functools
import math

import jax
import jax.numpy as jnp
from jax import lax
from jax.experimental import pallas as pl
from jax.experimental.pallas import tpu as pltpu
from jax.sharding import PartitionSpec as P


DK = 128
STRETCH = 64
F32 = jnp.float32
BF16 = jnp.bfloat16


def level_factor(level_num):
    token_count = STRETCH if level_num == 0 else STRETCH * 2 ** (level_num - 1)
    return 1.0 / math.sqrt(DK * token_count)


def swap(block, axis, stride):
    count = lax.axis_size(axis)
    return lax.ppermute(block, axis, [(i, i ^ stride) for i in range(count)])


VMEM = pl.BlockSpec(memory_space=pltpu.VMEM)
HBM = pl.BlockSpec(memory_space=pltpu.HBM)


def in_hbm(x):
    return pltpu.with_memory_space_constraint(x, pltpu.HBM)


def states(count, dtype=BF16):
    return jax.ShapeDtypeStruct((count, DK, DK), dtype)


def my_place():
    run, at = lax.axis_index("grp"), lax.axis_index("ctx")
    right = lax.shift_right_logical
    return run, at & 1, right(at, 1) & 3, right(at, 3), run * lax.axis_size("ctx") + at


def kernel_call(kernel, outs, operands, *, limit=16, flops=0, spaces=None, **more):
    moved = sum(x.size * x.dtype.itemsize for x in operands)
    out_specs = more.pop("out_specs", None) or jax.tree.map(lambda _: VMEM, outs)
    return pl.pallas_call(
        kernel,
        out_shape=outs,
        in_specs=spaces or [VMEM] * len(operands),
        out_specs=out_specs,
        compiler_params=pltpu.CompilerParams(vmem_limit_bytes=limit << 20),
        cost_estimate=pl.CostEstimate(flops=flops, transcendentals=0, bytes_accessed=moved),
        **more,
    )(*operands)


def lanes(head):
    start = head * DK
    return pl.ds(start if isinstance(start, int) else pl.multiple_of(start, DK), DK)


def state_kernel(flip, k_hbm, v_hbm, o_ref, k_ref, v_ref, sems):
    width = k_ref.shape[1]
    at = pl.ds(pl.multiple_of((my_place()[1] ^ flip) * width, width), width)
    copies = [
        pltpu.make_async_copy(src.at[:, at], dst, sems.at[i])
        for i, (src, dst) in enumerate(((k_hbm, k_ref), (v_hbm, v_ref)))
    ]
    for copy in copies:
        copy.start()
    for copy in copies:
        copy.wait()
    for n in range(o_ref.shape[0]):
        o_ref[n] = lax.dot_general(
            v_ref[:, lanes(n)], k_ref[:, lanes(n)], (((0,), (0,)), ((), ())), preferred_element_type=F32
        ).astype(BF16)


def half_states(flip, keys, values):
    rows, width = keys.shape
    buffer = pltpu.VMEM((rows, width // 2), BF16)
    return kernel_call(
        functools.partial(state_kernel, flip),
        states(width // DK // 2),
        [in_hbm(keys), in_hbm(values)],
        flops=rows * DK * width,
        spaces=[HBM, HBM],
        scratch_shapes=[buffer, buffer, pltpu.SemaphoreType.DMA((2,))],
    )


def local_kernel(q_hbm, k_hbm, v_hbm, w_ref, o_ref, q_ref, k_ref, v_ref, sems):
    rows, width = q_ref.shape
    heads = o_ref.shape[0]
    copies = []
    for part in range(2):
        at = pl.ds(part * width // 2, width // 2)
        pairs = ((q_hbm, q_ref), (k_hbm, k_ref), (v_hbm, v_ref))
        copies.append(
            [pltpu.make_async_copy(x.at[:, at], y.at[:, at], sems.at[part, i]) for i, (x, y) in enumerate(pairs)]
        )
    for copy in copies[0] + copies[1]:
        copy.start()
    tile = 2 * STRETCH
    key = lax.broadcasted_iota(jnp.int32, (tile, tile), 0)
    tok = lax.broadcasted_iota(jnp.int32, (tile, tile), 1)
    low = jnp.logical_and(tok >= STRETCH, key < STRETCH)
    same = jnp.logical_and(key <= tok, jnp.logical_not(low))
    for head in range(heads):
        if head % (heads // 2) == 0:
            for copy in copies[head // (heads // 2)]:
                copy.wait()
        at = lanes(head)
        value_t = v_ref[:, at].T
        for r in range(rows // tile):
            here = pl.ds(r * tile, tile)
            span = (r + 1) * tile

            def scale(level):
                return w_ref[level, pl.ds(head, 1), here] * level_factor(level)

            score = lax.dot_general(
                k_ref[pl.ds(0, span), at], q_ref[here, at], (((1,), (1,)), ((), ())),
                preferred_element_type=F32,
            )
            parts = []
            for c in range(r):
                parts.append(score[c * tile : (c + 1) * tile] * scale(1 + (r ^ c).bit_length()))
            weight = jnp.where(same, scale(0), jnp.where(low, scale(1), 0.0))
            parts.append(score[r * tile :] * weight)
            weighted = jnp.concatenate([p.astype(BF16) for p in parts], axis=0)
            o_ref[head, :, here] = jnp.dot(value_t[:, :span], weighted, preferred_element_type=F32)


def local_part(queries, keys, values, weights):
    rows, width = queries.shape
    buffer = pltpu.VMEM((rows, width), BF16)
    return kernel_call(
        local_kernel,
        jax.ShapeDtypeStruct((width // DK, DK, rows), F32),
        [in_hbm(queries), in_hbm(keys), in_hbm(values), weights],
        limit=32,
        flops=4 * rows * rows * width,
        spaces=[HBM, HBM, HBM, VMEM],
        scratch_shapes=[buffer, buffer, buffer, pltpu.SemaphoreType.DMA((2, 3))],
    )


def split_kernel(keep_ref, first_ref, one_ref, o_ref, rest_ref):
    partner = my_place()[2] ^ 2

    def total(n):
        return (keep_ref[n].astype(F32) + first_ref[n].astype(F32) + one_ref[n].astype(F32)).astype(BF16)

    o_ref[0] = total(partner)
    for d in range(1, 1 + rest_ref.shape[0]):
        rest_ref[d - 1] = total(partner ^ d)


def pick_kernel(keep_ref, first_ref, one_ref, two_ref, o_ref):
    n = my_place()[2]
    total = keep_ref[n].astype(F32) + first_ref[n].astype(F32) + one_ref[n].astype(F32) + two_ref[0].astype(F32)
    for g in range(o_ref.shape[0]):
        o_ref[g] = total.astype(BF16)


def sibling_sums(own, all_ref, o_ref, first):
    for b in range(all_ref.shape[0].bit_length() - 1):
        low = jnp.maximum(lax.shift_right_logical(own, b) - 1, 0) * 2**b
        total = all_ref[low].astype(F32)
        for i in range(1, 2**b):
            total = total + all_ref[low + i].astype(F32)
        o_ref[first + b] = total.astype(BF16)


def group_kernel(all_ref, late_ref, o_ref):
    sibling_sums(my_place()[3], all_ref, late_ref, 0)
    total = all_ref[0].astype(F32)
    for g in range(1, all_ref.shape[0]):
        total = total + all_ref[g].astype(F32)
    for r in range(o_ref.shape[0]):
        o_ref[r] = total.astype(BF16)


def run_kernel(all_ref, o_ref):
    sibling_sums(my_place()[0], all_ref, o_ref, 0)


def pack_kernel(keep_ref, first_ref, one_ref, two_ref, rest_ref, *refs):
    o_ref = refs[-1]
    half = keep_ref.shape[0]
    n = my_place()[2]
    o_ref[pl.ds(0, half)] = jnp.where(my_place()[1] == 1, first_ref[...], keep_ref[...])
    o_ref[pl.ds(half, half)] = one_ref[...]
    o_ref[2 * half + n] = two_ref[0]
    for d in range(1, half):
        o_ref[2 * half + (n ^ d)] = rest_ref[d - 1]
    start = 3 * half
    for ref in refs[:-1]:
        o_ref[pl.ds(start, ref.shape[0])] = ref[...]
        start += ref.shape[0]


def slot_head(slot):
    return my_place()[2] ^ (slot // 2 | slot % 2 * 2)


def add_levels(q_ref, w_ref, total, head, found, bits, local_bits):
    part = lax.dot_general(found, q_ref[:, lanes(head)], (((1,), (1,)), ((), ())), preferred_element_type=F32)
    for i, bit in enumerate(bits):
        level = 1 + local_bits + bit
        live = (lax.shift_right_logical(my_place()[4], bit) & 1) == 1
        gain = jnp.where(live, level_factor(level), 0.0)
        total = total + part[i * DK : (i + 1) * DK] * (w_ref[level, pl.ds(head, 1), :] * gain)
    return total


def send_out(o_ref, sems, out_hbm, copies, total, head):
    i = len(copies)
    o_ref[i] = total.astype(BF16).T
    copies.append(pltpu.make_async_copy(o_ref.at[i], out_hbm.at[:, lanes(head)], sems.at[i]))
    copies[-1].start()


def near_kernel(mid, late, local_bits, q_ref, a_ref, w_ref, mine_ref, their_ref, t_ref, out_hbm, o_ref, sems):
    half = a_ref.shape[0] // 2
    copies = []
    for other, ref in enumerate((mine_ref, their_ref)):
        side = my_place()[1] ^ other
        for slot in range(half):
            n = slot_head(slot)
            head = side * half + n
            found = [ref[level * half + n] for level in range(3)]
            found.append(ref[pl.ds(3 * half + slot * mid, mid)].reshape(mid * DK, DK))
            bits = 3 + mid
            if slot < 2:
                found.append(ref[pl.ds((3 + mid) * half + slot * late, late)].reshape(late * DK, DK))
                bits += late
            found = jnp.concatenate(found, axis=0)
            total = add_levels(q_ref, w_ref, a_ref[head], head, found, range(bits), local_bits)
            if slot < 2:
                send_out(o_ref, sems, out_hbm, copies, total, head)
            else:
                t_ref[other * (half - 2) + slot - 2] = total
    for copy in copies:
        copy.wait()


def far_kernel(other, mid, late, local_bits, q_ref, t_ref, w_ref, found_ref, before_hbm, out_hbm, o_ref, sems):
    count = t_ref.shape[0] // 2
    copies = []
    for i in range(count):
        head = (my_place()[1] ^ other) * 2 * count + slot_head(2 + i)
        found = found_ref[pl.ds(i * late, late)].reshape(late * DK, DK)
        bits = range(3 + mid, 3 + mid + late)
        total = add_levels(q_ref, w_ref, t_ref[other * count + i], head, found, bits, local_bits)
        send_out(o_ref, sems, out_hbm, copies, total, head)
    for copy in copies:
        copy.wait()


def attend(queries, keys, values, level_weights):
    rows, width = queries.shape
    heads = width // DK
    half = heads // 2
    local_bits = (rows // STRETCH).bit_length() - 1
    blocks = lax.axis_size("ctx")
    runs = lax.axis_size("grp")
    groups = blocks // 8
    send = half_states(1, keys, values)
    first = swap(send, "ctx", 1)
    keep = half_states(0, keys, values)
    running = keep.astype(F32) + first.astype(F32)
    one_z = swap(running.astype(BF16), "ctx", 2)
    ahead, rest = kernel_call(split_kernel, [states(1), states(half - 1)], [keep, first, one_z])
    two_z = swap(ahead, "ctx", 4)
    two_rest = swap(rest, "ctx", 4)
    picked = kernel_call(pick_kernel, states(groups), [keep, first, one_z, two_z])
    members = [[low + 8 * g for g in range(groups)] for low in range(8)]
    group_sums = lax.all_to_all(picked, "ctx", 0, 0, axis_index_groups=members, tiled=True)
    mid = groups.bit_length() - 1
    mid0, spread = kernel_call(group_kernel, [states(mid), states(runs)], [group_sums])
    run_states = lax.all_to_all(spread, "grp", 0, 0, tiled=True)

    mid1 = swap(mid0, "ctx", 4)
    mid23 = swap(jnp.concatenate([mid0, mid1], axis=0), "ctx", 2)
    late = runs.bit_length() - 1
    slot0 = kernel_call(run_kernel, states(late), [run_states])

    slot1 = swap(slot0, "ctx", 4)
    local = local_part(queries, keys, values, level_weights)
    slot23 = swap(jnp.concatenate([slot0, slot1], axis=0), "ctx", 2)
    mine = kernel_call(
        pack_kernel,
        states((3 + mid) * half + 2 * late),
        [keep, first, one_z, two_z, two_rest, mid0, mid1, mid23, slot0, slot1],
    )
    theirs = swap(mine, "ctx", 1)
    out_type = jax.ShapeDtypeStruct((rows, width), BF16)
    out_buffers = lambda n: [pltpu.VMEM((n, rows, DK), BF16), pltpu.SemaphoreType.DMA((n,))]
    total, out = kernel_call(
        functools.partial(near_kernel, mid, late, local_bits),
        [jax.ShapeDtypeStruct((heads - 4, DK, rows), F32), out_type],
        [queries, local, level_weights, mine, theirs],
        limit=24,
        flops=2 * rows * DK * DK * (heads * (3 + mid) + 4 * late),
        out_specs=[VMEM, HBM],
        scratch_shapes=out_buffers(4),
    )

    def far(other, found, out):
        return kernel_call(
            functools.partial(far_kernel, other, mid, late, local_bits),
            out_type,
            [queries, total, level_weights, found, out],
            flops=4 * rows * DK * DK * late,
            spaces=[VMEM] * 4 + [HBM],
            out_specs=HBM,
            scratch_shapes=out_buffers(2),
            input_output_aliases={4: 0},
        )

    their23 = swap(slot23, "ctx", 1)
    return far(1, their23, far(0, slot23, out))


def solution(mesh):
    return jax.shard_map(
        attend,
        mesh=mesh,
        in_specs=(
            P(("grp", "ctx"), None),
            P(("grp", "ctx"), None),
            P(("grp", "ctx"), None),
            P(None, None, ("grp", "ctx")),
        ),
        out_specs=P(("grp", "ctx"), None),
        check_vma=False,
    )
```

profile of v0, /device:TPU:1, one launch (start us, length us, event | category | flops | bytes accessed | tf_op | source)
XLA Modules:
  0.0 105.6 jit_solution(8018138725327350687)
XLA Ops:
  0.0 1.6 %shard_map.48 = bf16[4,128,128]{2,1,0:T(8,128)(2,1)S(1)} custom-call(bf16[512,1024]{1,0:T(8,128)(2,1)} %k_hbm.5, bf16[512,1024]{1,0:T(8,128)(2,1)} %v_hbm.5), custom_call_target="tpu_custom_call" | custom-call | flops 67108864 | bytes 2097152 | tf_op jit(solution)/shard_map/pallas_call | solution.py:49
  1.6 8.7 %collective-permute-start = (bf16[4,128,128]{2,1,0:T(8,128)(2,1)S(1)}, bf16[4,128,128]{2,1,0:T(8,128)(2,1)S(1)}, u32[]{:S(2)}, u32[]{:S(2)}) collective-permute-start(bf16[4,128,128]{2,1,0:T(8,128)(2,1)S(1)} %shard_map.48), channel_id=1, source_target_pairs={{0,1},{1,0},{2,3},{3,2},{4,5},{5,4},{6,7},{7,6},{8,9},{9,8},{10,11... | collective-permute-start | bytes 393224 | tf_op jit(solution)/shard_map/ppermute | solution.py:25
  10.3 1.6 %shard_map.47.keep_ref = bf16[4,128,128]{2,1,0:T(8,128)(2,1)S(1)} custom-call(bf16[512,1024]{1,0:T(8,128)(2,1)} %k_hbm.5, bf16[512,1024]{1,0:T(8,128)(2,1)} %v_hbm.5), custom_call_target="tpu_custom_call" | custom-call | flops 67108864 | bytes 2097152 | tf_op jit(solution)/shard_map/pallas_call | solution.py:49
  11.9 0.0 collective-permute-done.first_ref
  12.0 1.9 %collective-permute-start.1 = (bf16[4,128,128]{2,1,0:T(8,128)(2,1)S(1)}, bf16[4,128,128]{2,1,0:T(8,128)(2,1)S(1)}, u32[]{:S(2)}, u32[]{:S(2)}) collective-permute-start(bf16[4,128,128]{2,1,0:T(8,128)(2,1)S(1)} %add_convert_fusion), channel_id=1, source_target_pairs={{0,2},{1,3},{2,0},{3,1},{4,6},{5,7},{6,4},{7,5},{8,10},{9,11},{10,... | collective-permute-start | bytes 393224 | tf_op jit(solution)/shard_map/ppermute | solution.py:25
  13.9 5.0 %collective-permute-done.1.one_ref = bf16[4,128,128]{2,1,0:T(8,128)(2,1)S(1)} collective-permute-done((bf16[4,128,128]{2,1,0:T(8,128)(2,1)S(1)}, bf16[4,128,128]{2,1,0:T(8,128)(2,1)S(1)}, u32[]{:S(2)}, u32[]{:S(2)}) %collective-permute-start.1) | collective-permute-done | bytes 131104 | tf_op jit(solution)/shard_map/ppermute | solution.py:25
  18.9 0.1 shard_map.49
  19.0 1.9 %collective-permute-start.2 = (bf16[1,128,128]{2,1,0:T(8,128)(2,1)S(1)}, bf16[1,128,128]{2,1,0:T(8,128)(2,1)S(1)}, u32[]{:S(2)}, u32[]{:S(2)}) collective-permute-start(bf16[1,128,128]{2,1,0:T(8,128)(2,1)S(1)} %get-tuple-element.11), channel_id=1, source_target_pairs={{0,4},{1,5},{2,6},{3,7},{4,0},{5,1},{6,2},{7,3},{8,12},{9,13},{10,... | collective-permute-start | bytes 98312 | tf_op jit(solution)/shard_map/ppermute | solution.py:25
  20.9 4.0 %collective-permute-done.2.two_ref = bf16[1,128,128]{2,1,0:T(8,128)(2,1)S(1)} collective-permute-done((bf16[1,128,128]{2,1,0:T(8,128)(2,1)S(1)}, bf16[1,128,128]{2,1,0:T(8,128)(2,1)S(1)}, u32[]{:S(2)}, u32[]{:S(2)}) %collective-permute-start.2) | collective-permute-done | bytes 32800 | tf_op jit(solution)/shard_map/ppermute | solution.py:25
  24.9 21.1 %all_to_all.10.all_ref = bf16[4,128,128]{2,1,0:T(8,128)(2,1)S(1)} all-to-all(bf16[4,128,128]{2,1,0:T(8,128)(2,1)S(1)} %shard_map.50), channel_id=1, replica_groups={{0,8,16,24},{1,9,17,25},{2,10,18,26},{3,11,19,27},{4,12,20,28},{5,13,21..., dimensions={0} | all-to-all | bytes 262144 | tf_op jit(solution)/shard_map/all_to_all | solution.py:283
  46.0 0.9 shard_map.51
  46.9 0.0 copy-start.1
  46.9 6.9 %all-to-all-start.1 = ((bf16[16,128,128]{2,1,0:T(8,128)(2,1)}), bf16[16,128,128]{2,1,0:T(8,128)(2,1)S(1)}, u32[]{:S(2)}, u32[]{:S(2)}) async-start(bf16[16,128,128]{2,1,0:T(8,128)(2,1)} %get-tuple-element.14), calls=%async_computation.1 | async-start | bytes 1048576 | tf_op jit(solution)/shard_map/all_to_all | solution.py:286
  53.8 3.9 %collective-permute-start.4 = (bf16[2,128,128]{2,1,0:T(8,128)(2,1)S(1)}, bf16[2,128,128]{2,1,0:T(8,128)(2,1)S(1)}, u32[]{:S(2)}, u32[]{:S(2)}) collective-permute-start(bf16[2,128,128]{2,1,0:T(8,128)(2,1)S(1)} %get-tuple-element.13.refs_0_), channel_id=1, source_target_pairs={{0,4},{1,5},{2,6},{3,7},{4,0},{5,1},{6,2},{7,3},{8,12},{9,13},{10,... | collective-permute-start | bytes 196616 | tf_op jit(solution)/shard_map/ppermute | solution.py:25
  57.7 2.0 %collective-permute-done.4.refs_1_ = bf16[2,128,128]{2,1,0:T(8,128)(2,1)S(1)} collective-permute-done((bf16[2,128,128]{2,1,0:T(8,128)(2,1)S(1)}, bf16[2,128,128]{2,1,0:T(8,128)(2,1)S(1)}, u32[]{:S(2)}, u32[]{:S(2)}) %collective-permute-start.4) | collective-permute-done | bytes 65568 | tf_op jit(solution)/shard_map/ppermute | solution.py:25
  59.7 3.5 %collective-permute-start.5 = (bf16[4,128,128]{2,1,0:T(8,128)(2,1)S(1)}, bf16[4,128,128]{2,1,0:T(8,128)(2,1)S(1)}, u32[]{:S(2)}, u32[]{:S(2)}) collective-permute-start(bf16[4,128,128]{2,1,0:T(8,128)(2,1)S(1)} %pad_maximum_fusion.1), channel_id=1, source_target_pairs={{0,2},{1,3},{2,0},{3,1},{4,6},{5,7},{6,4},{7,5},{8,10},{9,11},{10,... | collective-permute-start | bytes 393224 | tf_op jit(solution)/shard_map/ppermute | solution.py:25
  63.1 0.0 all-to-all-done.1.all_ref
  63.2 0.1 shard_map.52.refs_3_
  63.2 3.5 %collective-permute-start.6 = (bf16[4,128,128]{2,1,0:T(8,128)(2,1)S(1)}, bf16[4,128,128]{2,1,0:T(8,128)(2,1)S(1)}, u32[]{:S(2)}, u32[]{:S(2)}) collective-permute-start(bf16[4,128,128]{2,1,0:T(8,128)(2,1)S(1)} %shard_map.52.refs_3_), channel_id=1, source_target_pairs={{0,4},{1,5},{2,6},{3,7},{4,0},{5,1},{6,2},{7,3},{8,12},{9,13},{10,... | collective-permute-start | bytes 393224 | tf_op jit(solution)/shard_map/ppermute | solution.py:25
  66.7 2.7 %collective-permute-start.3 = (bf16[3,128,128]{2,1,0:T(8,128)(2,1)S(1)}, bf16[3,128,128]{2,1,0:T(8,128)(2,1)S(1)}, u32[]{:S(2)}, u32[]{:S(2)}) collective-permute-start(bf16[3,128,128]{2,1,0:T(8,128)(2,1)S(1)} %get-tuple-element.12), channel_id=1, source_target_pairs={{0,4},{1,5},{2,6},{3,7},{4,0},{5,1},{6,2},{7,3},{8,12},{9,13},{10,... | collective-permute-start | bytes 294920 | tf_op jit(solution)/shard_map/ppermute | solution.py:25
  69.4 4.6 %collective-permute-done.3.rest_ref = bf16[3,128,128]{2,1,0:T(8,128)(2,1)S(1)} collective-permute-done((bf16[3,128,128]{2,1,0:T(8,128)(2,1)S(1)}, bf16[3,128,128]{2,1,0:T(8,128)(2,1)S(1)}, u32[]{:S(2)}, u32[]{:S(2)}) %collective-permute-start.3) | collective-permute-done | bytes 98336 | tf_op jit(solution)/shard_map/ppermute | solution.py:25
  74.0 0.0 collective-permute-done.5.refs_2_
  74.1 0.0 collective-permute-done.6.refs_4_
  74.1 0.1 shard_map.53.mine_ref
  74.1 8.5 %collective-permute-start.7 = (bf16[28,128,128]{2,1,0:T(8,128)(2,1)S(1)}, bf16[28,128,128]{2,1,0:T(8,128)(2,1)S(1)}, u32[]{:S(2)}, u32[]{:S(2)}) collective-permute-start(bf16[28,128,128]{2,1,0:T(8,128)(2,1)S(1)} %shard_map.53.mine_ref), channel_id=1, source_target_pairs={{0,1},{1,0},{2,3},{3,2},{4,5},{5,4},{6,7},{7,6},{8,9},{9,8},{10,11... | collective-permute-start | bytes 2752520 | tf_op jit(solution)/shard_map/ppermute | solution.py:25
  82.7 0.0 copy-start
  82.7 3.4 %collective-permute-start.8 = (bf16[8,128,128]{2,1,0:T(8,128)(2,1)S(1)}, bf16[8,128,128]{2,1,0:T(8,128)(2,1)S(1)}, u32[]{:S(2)}, u32[]{:S(2)}) collective-permute-start(bf16[8,128,128]{2,1,0:T(8,128)(2,1)S(1)} %pad_maximum_fusion), channel_id=1, source_target_pairs={{0,2},{1,3},{2,0},{3,1},{4,6},{5,7},{6,4},{7,5},{8,10},{9,11},{10,... | collective-permute-start | bytes 786440 | tf_op jit(solution)/shard_map/ppermute | solution.py:25
  86.1 6.5 %collective-permute-done.8.found_ref = bf16[8,128,128]{2,1,0:T(8,128)(2,1)S(1)} collective-permute-done((bf16[8,128,128]{2,1,0:T(8,128)(2,1)S(1)}, bf16[8,128,128]{2,1,0:T(8,128)(2,1)S(1)}, u32[]{:S(2)}, u32[]{:S(2)}) %collective-permute-start.8) | collective-permute-done | bytes 262176 | tf_op jit(solution)/shard_map/ppermute | solution.py:25
  92.6 2.8 %collective-permute-start.9 = (bf16[8,128,128]{2,1,0:T(8,128)(2,1)S(1)}, bf16[8,128,128]{2,1,0:T(8,128)(2,1)S(1)}, u32[]{:S(2)}, u32[]{:S(2)}) collective-permute-start(bf16[8,128,128]{2,1,0:T(8,128)(2,1)S(1)} %collective-permute-done.8.found_ref), channel_id=1, source_target_pairs={{0,1},{1,0},{2,3},{3,2},{4,5},{5,4},{6,7},{7,6},{8,9},{9,8},{10,11... | collective-permute-start | bytes 786440 | tf_op jit(solution)/shard_map/ppermute | solution.py:25
  95.4 0.0 copy-done.1
  95.4 5.0 %shard_map.46.a_ref = f32[8,128,512]{2,1,0:T(8,128)S(1)} custom-call(bf16[512,1024]{1,0:T(8,128)(2,1)} %q_ref.5, bf16[512,1024]{1,0:T(8,128)(2,1)} %k_hbm.5, bf16[512,1024]{1,0:T(8,128)(2,1)} %v_hbm.5, f32[13,8,512]{2,1,0:T(8,128)S(1)} %copy-done.1), custom_call_target="tpu_custom_call" | custom-call | flops 1073741824 | bytes 3358720 | tf_op jit(solution)/shard_map/pallas_call | solution.py:49
  100.4 0.0 collective-permute-done.7.their_ref
  100.4 0.0 copy-done
  100.4 2.8 %shard_map.54 = (f32[4,128,512]{2,1,0:T(8,128)S(1)}, bf16[512,1024]{1,0:T(8,128)(2,1)}) custom-call(bf16[512,1024]{1,0:T(8,128)(2,1)S(1)} %copy-done, f32[8,128,512]{2,1,0:T(8,128)S(1)} %shard_map.46.a_ref, f32[13,8,512]{2,1,0:T(8,128)S(1)} %copy-done.1, bf16[28,128,128]{2,1,0:T(8,128)(2,1)S(1)} %shard_map.53.mine_ref, ...), custom_call_target="tpu_custom_call" | custom-call | flops 939524096 | bytes 5193728 | tf_op jit(solution)/shard_map/pallas_call | solution.py:49
  103.2 1.2 %shard_map.55.before_hbm = bf16[512,1024]{1,0:T(8,128)(2,1)} custom-call(bf16[512,1024]{1,0:T(8,128)(2,1)S(1)} %copy-done, f32[4,128,512]{2,1,0:T(8,128)S(1)} %get-tuple-element.15.t_ref, f32[13,8,512]{2,1,0:T(8,128)S(1)} %copy-done.1, bf16[8,128,128]{2,1,0:T(8,128)(2,1)S(1)} %collective-permute-done.8.found_ref, ...), custom_call_target="tpu_custom_call", output_to_operand_aliasing={{}: (4, {})} | custom-call | flops 134217728 | bytes 3620864 | tf_op jit(solution)/shard_map/pallas_call | solution.py:49
  104.4 0.0 collective-permute-done.9.found_ref
  104.4 1.2 %shard_map.56 = bf16[512,1024]{1,0:T(8,128)(2,1)} custom-call(bf16[512,1024]{1,0:T(8,128)(2,1)S(1)} %copy-done, f32[4,128,512]{2,1,0:T(8,128)S(1)} %get-tuple-element.15.t_ref, f32[13,8,512]{2,1,0:T(8,128)S(1)} %copy-done.1, bf16[8,128,128]{2,1,0:T(8,128)(2,1)S(1)} %collective-permute-done.9.found_ref, ...), custom_call_target="tpu_custom_call", output_to_operand_aliasing={{}: (4, {})} | custom-call | flops 134217728 | bytes 3620864 | tf_op jit(solution)/shard_map/pallas_call | solution.py:49
  (4 shorter events, 0.1 us)
Async XLA Ops:
  1.6 10.3 %collective-permute-start = (bf16[4,128,128]{2,1,0:T(8,128)(2,1)S(1)}, bf16[4,128,128]{2,1,0:T(8,128)(2,1)S(1)}, u32[]{:S(2)}, u32[]{:S(2)}) collective-permute-start(bf16[4,128,128]{2,1,0:T(8,128)(2,1)S(1)} %shard_map.48), channel_id=1, source_target_pairs={{0,1},{1,0},{2,3},{3,2},{4,5},{5,4},{6,7},{7,6},{8,9},{9,8},{10,11... | collective-permute-start | bytes 393224 | tf_op jit(solution)/shard_map/ppermute | solution.py:25
  12.0 6.9 %collective-permute-start.1 = (bf16[4,128,128]{2,1,0:T(8,128)(2,1)S(1)}, bf16[4,128,128]{2,1,0:T(8,128)(2,1)S(1)}, u32[]{:S(2)}, u32[]{:S(2)}) collective-permute-start(bf16[4,128,128]{2,1,0:T(8,128)(2,1)S(1)} %add_convert_fusion), channel_id=1, source_target_pairs={{0,2},{1,3},{2,0},{3,1},{4,6},{5,7},{6,4},{7,5},{8,10},{9,11},{10,... | collective-permute-start | bytes 393224 | tf_op jit(solution)/shard_map/ppermute | solution.py:25
  19.0 5.9 %collective-permute-start.2 = (bf16[1,128,128]{2,1,0:T(8,128)(2,1)S(1)}, bf16[1,128,128]{2,1,0:T(8,128)(2,1)S(1)}, u32[]{:S(2)}, u32[]{:S(2)}) collective-permute-start(bf16[1,128,128]{2,1,0:T(8,128)(2,1)S(1)} %get-tuple-element.11), channel_id=1, source_target_pairs={{0,4},{1,5},{2,6},{3,7},{4,0},{5,1},{6,2},{7,3},{8,12},{9,13},{10,... | collective-permute-start | bytes 98312 | tf_op jit(solution)/shard_map/ppermute | solution.py:25
  46.9 48.5 %copy-start.1 = (f32[13,8,512]{2,1,0:T(8,128)S(1)}, f32[13,8,512]{2,1,0:T(8,128)}, u32[]{:S(2)}) copy-start(f32[13,8,512]{2,1,0:T(8,128)} %w_ref.7) | copy-start | bytes 638980
  46.9 16.3 %all-to-all-start.1 = ((bf16[16,128,128]{2,1,0:T(8,128)(2,1)}), bf16[16,128,128]{2,1,0:T(8,128)(2,1)S(1)}, u32[]{:S(2)}, u32[]{:S(2)}) async-start(bf16[16,128,128]{2,1,0:T(8,128)(2,1)} %get-tuple-element.14), calls=%async_computation.1 | async-start | bytes 1048576 | tf_op jit(solution)/shard_map/all_to_all | solution.py:286
  53.8 5.9 %collective-permute-start.4 = (bf16[2,128,128]{2,1,0:T(8,128)(2,1)S(1)}, bf16[2,128,128]{2,1,0:T(8,128)(2,1)S(1)}, u32[]{:S(2)}, u32[]{:S(2)}) collective-permute-start(bf16[2,128,128]{2,1,0:T(8,128)(2,1)S(1)} %get-tuple-element.13.refs_0_), channel_id=1, source_target_pairs={{0,4},{1,5},{2,6},{3,7},{4,0},{5,1},{6,2},{7,3},{8,12},{9,13},{10,... | collective-permute-start | bytes 196616 | tf_op jit(solution)/shard_map/ppermute | solution.py:25
  59.7 14.4 %collective-permute-start.5 = (bf16[4,128,128]{2,1,0:T(8,128)(2,1)S(1)}, bf16[4,128,128]{2,1,0:T(8,128)(2,1)S(1)}, u32[]{:S(2)}, u32[]{:S(2)}) collective-permute-start(bf16[4,128,128]{2,1,0:T(8,128)(2,1)S(1)} %pad_maximum_fusion.1), channel_id=1, source_target_pairs={{0,2},{1,3},{2,0},{3,1},{4,6},{5,7},{6,4},{7,5},{8,10},{9,11},{10,... | collective-permute-start | bytes 393224 | tf_op jit(solution)/shard_map/ppermute | solution.py:25
  63.2 10.8 %collective-permute-start.6 = (bf16[4,128,128]{2,1,0:T(8,128)(2,1)S(1)}, bf16[4,128,128]{2,1,0:T(8,128)(2,1)S(1)}, u32[]{:S(2)}, u32[]{:S(2)}) collective-permute-start(bf16[4,128,128]{2,1,0:T(8,128)(2,1)S(1)} %shard_map.52.refs_3_), channel_id=1, source_target_pairs={{0,4},{1,5},{2,6},{3,7},{4,0},{5,1},{6,2},{7,3},{8,12},{9,13},{10,... | collective-permute-start | bytes 393224 | tf_op jit(solution)/shard_map/ppermute | solution.py:25
  66.7 7.3 %collective-permute-start.3 = (bf16[3,128,128]{2,1,0:T(8,128)(2,1)S(1)}, bf16[3,128,128]{2,1,0:T(8,128)(2,1)S(1)}, u32[]{:S(2)}, u32[]{:S(2)}) collective-permute-start(bf16[3,128,128]{2,1,0:T(8,128)(2,1)S(1)} %get-tuple-element.12), channel_id=1, source_target_pairs={{0,4},{1,5},{2,6},{3,7},{4,0},{5,1},{6,2},{7,3},{8,12},{9,13},{10,... | collective-permute-start | bytes 294920 | tf_op jit(solution)/shard_map/ppermute | solution.py:25
  74.1 26.2 %collective-permute-start.7 = (bf16[28,128,128]{2,1,0:T(8,128)(2,1)S(1)}, bf16[28,128,128]{2,1,0:T(8,128)(2,1)S(1)}, u32[]{:S(2)}, u32[]{:S(2)}) collective-permute-start(bf16[28,128,128]{2,1,0:T(8,128)(2,1)S(1)} %shard_map.53.mine_ref), channel_id=1, source_target_pairs={{0,1},{1,0},{2,3},{3,2},{4,5},{5,4},{6,7},{7,6},{8,9},{9,8},{10,11... | collective-permute-start | bytes 2752520 | tf_op jit(solution)/shard_map/ppermute | solution.py:25
  82.7 17.7 %copy-start = (bf16[512,1024]{1,0:T(8,128)(2,1)S(1)}, bf16[512,1024]{1,0:T(8,128)(2,1)}, u32[]{:S(2)}) copy-start(bf16[512,1024]{1,0:T(8,128)(2,1)} %q_ref.5) | copy-start | bytes 3145732
  82.7 9.9 %collective-permute-start.8 = (bf16[8,128,128]{2,1,0:T(8,128)(2,1)S(1)}, bf16[8,128,128]{2,1,0:T(8,128)(2,1)S(1)}, u32[]{:S(2)}, u32[]{:S(2)}) collective-permute-start(bf16[8,128,128]{2,1,0:T(8,128)(2,1)S(1)} %pad_maximum_fusion), channel_id=1, source_target_pairs={{0,2},{1,3},{2,0},{3,1},{4,6},{5,7},{6,4},{7,5},{8,10},{9,11},{10,... | collective-permute-start | bytes 786440 | tf_op jit(solution)/shard_map/ppermute | solution.py:25
  92.6 11.8 %collective-permute-start.9 = (bf16[8,128,128]{2,1,0:T(8,128)(2,1)S(1)}, bf16[8,128,128]{2,1,0:T(8,128)(2,1)S(1)}, u32[]{:S(2)}, u32[]{:S(2)}) collective-permute-start(bf16[8,128,128]{2,1,0:T(8,128)(2,1)S(1)} %collective-permute-done.8.found_ref), channel_id=1, source_target_pairs={{0,1},{1,0},{2,3},{3,2},{4,5},{5,4},{6,7},{7,6},{8,9},{9,8},{10,11... | collective-permute-start | bytes 786440 | tf_op jit(solution)/shard_map/ppermute | solution.py:25
where the time goes:
time: 106 us
  starting transfers between devices  47.7 us (45%)
  waiting for transfers between devices  22.1 us (21%)
  blocking collectives  21.1 us (20%)
  Pallas kernels  14.4 us (14%)
    ppermute x10, starting transfers between devices, swap(): return lax.ppermute(block, axis, [(i, i ^ stride) for i in range(count)])  40.8 us
    ppermute x10, waiting for transfers between devices, swap(): return lax.ppermute(block, axis, [(i, i ^ stride) for i in range(count)])  22.1 us
    all_to_all x1, blocking collectives, attend(): lax.all_to_all(picked, 'ctx', 0, 0, axis_index_groups=members, tiled=True)  21.1 us
    pallas_call x11, Pallas kernels, kernel_call(): pl.pallas_call(kernel, out_shape=outs, in_specs=spaces or [VMEM] * len(op...  14.4 us
    all_to_all x1, starting transfers between devices, attend(): run_states = lax.all_to_all(spread, 'grp', 0, 0, tiled=True)  6.88 us
  transfers between devices with their start and end apart: 11, of which 5 were waited for; matrix products, arithmetic and copies ran while one was open for 0% of the time, Pallas kernels for 10%

commit v1 on v0

--- a/solution.py
+++ b/solution.py
@@ -92,7 +92,7 @@
     )
 
 
-def local_kernel(q_hbm, k_hbm, v_hbm, w_ref, o_ref, q_ref, k_ref, v_ref, sems):
+def local_kernel(q_hbm, k_hbm, v_hbm, w_ref, o_hbm, q_ref, k_ref, v_ref, o_ref, sems, out_sems):
     rows, width = q_ref.shape
     heads = o_ref.shape[0]
     copies = []
@@ -109,6 +109,7 @@
     tok = lax.broadcasted_iota(jnp.int32, (tile, tile), 1)
     low = jnp.logical_and(tok >= STRETCH, key < STRETCH)
     same = jnp.logical_and(key <= tok, jnp.logical_not(low))
+    results = []
     for head in range(heads):
         if head % (heads // 2) == 0:
             for copy in copies[head // (heads // 2)]:
@@ -133,36 +134,56 @@
             parts.append(score[r * tile :] * weight)
             weighted = jnp.concatenate([p.astype(BF16) for p in parts], axis=0)
             o_ref[head, :, here] = jnp.dot(value_t[:, :span], weighted, preferred_element_type=F32)
+        results.append(pltpu.make_async_copy(o_ref.at[head], o_hbm.at[head], out_sems.at[head]))
+        results[-1].start()
+    for copy in results:
+        copy.wait()
 
 
 def local_part(queries, keys, values, weights):
     rows, width = queries.shape
     buffer = pltpu.VMEM((rows, width), BF16)
+    heads = width // DK
     return kernel_call(
         local_kernel,
-        jax.ShapeDtypeStruct((width // DK, DK, rows), F32),
+        pltpu.HBM((heads, DK, rows), F32),
         [in_hbm(queries), in_hbm(keys), in_hbm(values), weights],
         limit=32,
         flops=4 * rows * rows * width,
         spaces=[HBM, HBM, HBM, VMEM],
-        scratch_shapes=[buffer, buffer, buffer, pltpu.SemaphoreType.DMA((2, 3))],
+        out_specs=HBM,
+        scratch_shapes=[
+            buffer,
+            buffer,
+            buffer,
+            pltpu.VMEM((heads, DK, rows), F32),
+            pltpu.SemaphoreType.DMA((2, 3)),
+            pltpu.SemaphoreType.DMA((heads,)),
+        ],
     )
 
 
-def split_kernel(keep_ref, first_ref, one_ref, o_ref, rest_ref):
-    partner = my_place()[2] ^ 2
-
-    def total(n):
-        return (keep_ref[n].astype(F32) + first_ref[n].astype(F32) + one_ref[n].astype(F32)).astype(BF16)
-
-    o_ref[0] = total(partner)
-    for d in range(1, 1 + rest_ref.shape[0]):
-        rest_ref[d - 1] = total(partner ^ d)
+def pair_kernel(keep_ref, first_ref, o_ref, rest_ref):
+    partner = my_place()[2] ^ 1
+    for i, d in enumerate((0, 2, 1, 3)):
+        total = keep_ref[partner ^ d].astype(F32) + first_ref[partner ^ d].astype(F32)
+        (o_ref if i < 2 else rest_ref)[i % 2] = total.astype(BF16)
+
+
+def ahead_kernel(keep_ref, first_ref, one_ref, o_ref):
+    n = my_place()[2] ^ 2
+    o_ref[0] = (keep_ref[n].astype(F32) + first_ref[n].astype(F32) + one_ref[1].astype(F32)).astype(BF16)
+
+
+def rest_kernel(keep_ref, first_ref, one_ref, other_ref, o_ref):
+    n = my_place()[2]
+    for i, (d, got) in enumerate(((3, other_ref[1]), (0, one_ref[0]), (1, other_ref[0]))):
+        o_ref[i] = (keep_ref[n ^ d].astype(F32) + first_ref[n ^ d].astype(F32) + got.astype(F32)).astype(BF16)
 
 
 def pick_kernel(keep_ref, first_ref, one_ref, two_ref, o_ref):
     n = my_place()[2]
-    total = keep_ref[n].astype(F32) + first_ref[n].astype(F32) + one_ref[n].astype(F32) + two_ref[0].astype(F32)
+    total = keep_ref[n].astype(F32) + first_ref[n].astype(F32) + one_ref[0].astype(F32) + two_ref[0].astype(F32)
     for g in range(o_ref.shape[0]):
         o_ref[g] = total.astype(BF16)
 
@@ -189,12 +210,14 @@
     sibling_sums(my_place()[0], all_ref, o_ref, 0)
 
 
-def pack_kernel(keep_ref, first_ref, one_ref, two_ref, rest_ref, *refs):
+def pack_kernel(keep_ref, first_ref, one_ref, other_ref, two_ref, rest_ref, *refs):
     o_ref = refs[-1]
     half = keep_ref.shape[0]
     n = my_place()[2]
     o_ref[pl.ds(0, half)] = jnp.where(my_place()[1] == 1, first_ref[...], keep_ref[...])
-    o_ref[pl.ds(half, half)] = one_ref[...]
+    for i in range(2):
+        o_ref[half + (n ^ 2 * i)] = one_ref[i]
+        o_ref[half + (n ^ 1 ^ 2 * i)] = other_ref[i]
     o_ref[2 * half + n] = two_ref[0]
     for d in range(1, half):
         o_ref[2 * half + (n ^ d)] = rest_ref[d - 1]
@@ -225,38 +248,43 @@
     copies[-1].start()
 
 
-def near_kernel(mid, late, local_bits, q_ref, a_ref, w_ref, mine_ref, their_ref, t_ref, out_hbm, o_ref, sems):
-    half = a_ref.shape[0] // 2
+def near_kernel(other, mid, late, local_bits, q_ref, a_hbm, w_ref, found_ref, *refs):
+    t_ref, out_hbm, o_ref, sems, a_ref, a_sems = refs[-6:]
+    half = a_ref.shape[0]
+    locals_ = []
+    for slot in range(half):
+        head = (my_place()[1] ^ other) * half + slot_head(slot)
+        locals_.append(pltpu.make_async_copy(a_hbm.at[head], a_ref.at[slot], a_sems.at[slot]))
+        locals_[-1].start()
     copies = []
-    for other, ref in enumerate((mine_ref, their_ref)):
-        side = my_place()[1] ^ other
-        for slot in range(half):
-            n = slot_head(slot)
-            head = side * half + n
-            found = [ref[level * half + n] for level in range(3)]
-            found.append(ref[pl.ds(3 * half + slot * mid, mid)].reshape(mid * DK, DK))
-            bits = 3 + mid
-            if slot < 2:
-                found.append(ref[pl.ds((3 + mid) * half + slot * late, late)].reshape(late * DK, DK))
-                bits += late
-            found = jnp.concatenate(found, axis=0)
-            total = add_levels(q_ref, w_ref, a_ref[head], head, found, range(bits), local_bits)
-            if slot < 2:
-                send_out(o_ref, sems, out_hbm, copies, total, head)
-            else:
-                t_ref[other * (half - 2) + slot - 2] = total
+    for slot in range(half):
+        n = slot_head(slot)
+        head = (my_place()[1] ^ other) * half + n
+        locals_[slot].wait()
+        found = [found_ref[level * half + n] for level in range(3)]
+        found.append(found_ref[pl.ds(3 * half + slot * mid, mid)].reshape(mid * DK, DK))
+        bits = 3 + mid
+        if slot < 2:
+            found.append(found_ref[pl.ds((3 + mid) * half + slot * late, late)].reshape(late * DK, DK))
+            bits += late
+        found = jnp.concatenate(found, axis=0)
+        total = add_levels(q_ref, w_ref, a_ref[slot], head, found, range(bits), local_bits)
+        if slot < 2:
+            send_out(o_ref, sems, out_hbm, copies, total, head)
+        else:
+            t_ref[slot - 2] = total
     for copy in copies:
         copy.wait()
 
 
 def far_kernel(other, mid, late, local_bits, q_ref, t_ref, w_ref, found_ref, before_hbm, out_hbm, o_ref, sems):
-    count = t_ref.shape[0] // 2
+    count = t_ref.shape[0]
     copies = []
     for i in range(count):
         head = (my_place()[1] ^ other) * 2 * count + slot_head(2 + i)
         found = found_ref[pl.ds(i * late, late)].reshape(late * DK, DK)
         bits = range(3 + mid, 3 + mid + late)
-        total = add_levels(q_ref, w_ref, t_ref[other * count + i], head, found, bits, local_bits)
+        total = add_levels(q_ref, w_ref, t_ref[i], head, found, bits, local_bits)
         send_out(o_ref, sems, out_hbm, copies, total, head)
     for copy in copies:
         copy.wait()
@@ -273,11 +301,14 @@
     send = half_states(1, keys, values)
     first = swap(send, "ctx", 1)
     keep = half_states(0, keys, values)
-    running = keep.astype(F32) + first.astype(F32)
-    one_z = swap(running.astype(BF16), "ctx", 2)
-    ahead, rest = kernel_call(split_kernel, [states(1), states(half - 1)], [keep, first, one_z])
+    pair, pair_rest = kernel_call(pair_kernel, [states(2), states(half - 2)], [keep, first])
+    one_z = swap(pair, "ctx", 2)
+    one_rest = swap(pair_rest, "ctx", 2)
+    ahead = kernel_call(ahead_kernel, states(1), [keep, first, one_z])
     two_z = swap(ahead, "ctx", 4)
+    rest = kernel_call(rest_kernel, states(half - 1), [keep, first, one_z, one_rest])
     two_rest = swap(rest, "ctx", 4)
+    local = local_part(queries, keys, values, level_weights)
     picked = kernel_call(pick_kernel, states(groups), [keep, first, one_z, two_z])
     members = [[low + 8 * g for g in range(groups)] for low in range(8)]
     group_sums = lax.all_to_all(picked, "ctx", 0, 0, axis_index_groups=members, tiled=True)
@@ -291,31 +322,34 @@
     slot0 = kernel_call(run_kernel, states(late), [run_states])
 
     slot1 = swap(slot0, "ctx", 4)
-    local = local_part(queries, keys, values, level_weights)
     slot23 = swap(jnp.concatenate([slot0, slot1], axis=0), "ctx", 2)
     mine = kernel_call(
         pack_kernel,
         states((3 + mid) * half + 2 * late),
-        [keep, first, one_z, two_z, two_rest, mid0, mid1, mid23, slot0, slot1],
+        [keep, first, one_z, one_rest, two_z, two_rest, mid0, mid1, mid23, slot0, slot1],
     )
     theirs = swap(mine, "ctx", 1)
     out_type = jax.ShapeDtypeStruct((rows, width), BF16)
     out_buffers = lambda n: [pltpu.VMEM((n, rows, DK), BF16), pltpu.SemaphoreType.DMA((n,))]
-    total, out = kernel_call(
-        functools.partial(near_kernel, mid, late, local_bits),
-        [jax.ShapeDtypeStruct((heads - 4, DK, rows), F32), out_type],
-        [queries, local, level_weights, mine, theirs],
-        limit=24,
-        flops=2 * rows * DK * DK * (heads * (3 + mid) + 4 * late),
-        out_specs=[VMEM, HBM],
-        scratch_shapes=out_buffers(4),
-    )
-
-    def far(other, found, out):
+
+    def near(other, found, before):
+        return kernel_call(
+            functools.partial(near_kernel, other, mid, late, local_bits),
+            [jax.ShapeDtypeStruct((half - 2, DK, rows), F32), out_type],
+            [queries, in_hbm(local), level_weights, found, *before],
+            limit=24,
+            flops=2 * rows * DK * DK * (half * (3 + mid) + 2 * late),
+            spaces=[VMEM, HBM, VMEM, VMEM] + [HBM] * len(before),
+            out_specs=[VMEM, HBM],
+            scratch_shapes=out_buffers(2) + [pltpu.VMEM((half, DK, rows), F32), pltpu.SemaphoreType.DMA((half,))],
+            input_output_aliases={4: 1} if before else {},
+        )
+
+    def far(other, total, found, before):
         return kernel_call(
             functools.partial(far_kernel, other, mid, late, local_bits),
             out_type,
-            [queries, total, level_weights, found, out],
+            [queries, total, level_weights, found, before],
             flops=4 * rows * DK * DK * late,
             spaces=[VMEM] * 4 + [HBM],
             out_specs=HBM,
@@ -323,8 +357,11 @@
             input_output_aliases={4: 0},
         )
 
+    own_total, out = near(0, mine, [])
+    other_total, out = near(1, theirs, [out])
     their23 = swap(slot23, "ctx", 1)
-    return far(1, their23, far(0, slot23, out))
+    out = far(0, own_total, slot23, out)
+    return far(1, other_total, their23, out)
 
 
 def solution(mesh):

time: 106 us -> 108 us (1.019)
  Pallas kernels: 14.4 us -> 18.1 us
  waiting for transfers between devices: 22.1 us -> 18.5 us
  starting transfers between devices: 47.7 us -> 49.7 us
    pallas_call x11 -> x14, Pallas kernels: 14.4 us -> 18.1 us  [kernel_call(): pl.pallas_call(kernel, out_shape=outs, in_specs=spaces or [VMEM] * len(op...]
    ppermute x10 -> x11, waiting for transfers between devices: 22.1 us -> 18.5 us  [swap(): return lax.ppermute(block, axis, [(i, i ^ stride) for i in range(count)])]
    ppermute x10 -> x11, starting transfers between devices: 40.8 us -> 43 us  [swap(): return lax.ppermute(block, axis, [(i, i ^ stride) for i in range(count)])]
  transfers between devices with their start and end apart: 11 -> 12, of which waited for: 5 -> 5; matrix products, arithmetic and copies ran while one was open for 0% -> 0% of each run, Pallas kernels for 10% -> 13%
where the time goes in v1:
time: 108 us
  starting transfers between devices  49.7 us (46%)
  blocking collectives  21.1 us (20%)
  waiting for transfers between devices  18.5 us (17%)
  Pallas kernels  18.1 us (17%)
    ppermute x11, starting transfers between devices, swap(): return lax.ppermute(block, axis, [(i, i ^ stride) for i in range(count)])  43 us
    all_to_all x1, blocking collectives, attend(): lax.all_to_all(picked, 'ctx', 0, 0, axis_index_groups=members, tiled=True)  21.1 us
    ppermute x11, waiting for transfers between devices, swap(): return lax.ppermute(block, axis, [(i, i ^ stride) for i in range(count)])  18.5 us
    pallas_call x14, Pallas kernels, kernel_call(): pl.pallas_call(kernel, out_shape=outs, in_specs=spaces or [VMEM] * len(op...  18.1 us
    all_to_all x1, starting transfers between devices, attend(): run_states = lax.all_to_all(spread, 'grp', 0, 0, tiled=True)  6.75 us
  transfers between devices with their start and end apart: 12, of which 5 were waited for; matrix products, arithmetic and copies ran while one was open for 0% of the time, Pallas kernels for 13%

profile of v1, /device:TPU:1, one launch (start us, length us, event | category | flops | bytes accessed | tf_op | source)
XLA Modules:
  0.0 107.8 jit_solution(3902950656465745617)
XLA Ops:
  0.0 1.6 %shard_map.48 = bf16[4,128,128]{2,1,0:T(8,128)(2,1)S(1)} custom-call(bf16[512,1024]{1,0:T(8,128)(2,1)} %k_hbm.5, bf16[512,1024]{1,0:T(8,128)(2,1)} %v_hbm.5), custom_call_target="tpu_custom_call" | custom-call | flops 67108864 | bytes 2097152 | tf_op jit(solution)/shard_map/pallas_call | solution.py:49
  1.6 8.7 %collective-permute-start = (bf16[4,128,128]{2,1,0:T(8,128)(2,1)S(1)}, bf16[4,128,128]{2,1,0:T(8,128)(2,1)S(1)}, u32[]{:S(2)}, u32[]{:S(2)}) collective-permute-start(bf16[4,128,128]{2,1,0:T(8,128)(2,1)S(1)} %shard_map.48), channel_id=1, source_target_pairs={{0,1},{1,0},{2,3},{3,2},{4,5},{5,4},{6,7},{7,6},{8,9},{9,8},{10,11... | collective-permute-start | bytes 393224 | tf_op jit(solution)/shard_map/ppermute | solution.py:25
  10.3 1.6 %shard_map.47.keep_ref = bf16[4,128,128]{2,1,0:T(8,128)(2,1)S(1)} custom-call(bf16[512,1024]{1,0:T(8,128)(2,1)} %k_hbm.5, bf16[512,1024]{1,0:T(8,128)(2,1)} %v_hbm.5), custom_call_target="tpu_custom_call" | custom-call | flops 67108864 | bytes 2097152 | tf_op jit(solution)/shard_map/pallas_call | solution.py:49
  11.9 0.0 collective-permute-done.first_ref
  12.0 1.9 %collective-permute-start.1 = (bf16[2,128,128]{2,1,0:T(8,128)(2,1)S(1)}, bf16[2,128,128]{2,1,0:T(8,128)(2,1)S(1)}, u32[]{:S(2)}, u32[]{:S(2)}) collective-permute-start(bf16[2,128,128]{2,1,0:T(8,128)(2,1)S(1)} %get-tuple-element.13), channel_id=1, source_target_pairs={{0,2},{1,3},{2,0},{3,1},{4,6},{5,7},{6,4},{7,5},{8,10},{9,11},{10,... | collective-permute-start | bytes 196616 | tf_op jit(solution)/shard_map/ppermute | solution.py:25
  13.9 3.6 %collective-permute-done.1.one_ref = bf16[2,128,128]{2,1,0:T(8,128)(2,1)S(1)} collective-permute-done((bf16[2,128,128]{2,1,0:T(8,128)(2,1)S(1)}, bf16[2,128,128]{2,1,0:T(8,128)(2,1)S(1)}, u32[]{:S(2)}, u32[]{:S(2)}) %collective-permute-start.1) | collective-permute-done | bytes 65568 | tf_op jit(solution)/shard_map/ppermute | solution.py:25
  17.5 1.9 %collective-permute-start.3 = (bf16[1,128,128]{2,1,0:T(8,128)(2,1)S(1)}, bf16[1,128,128]{2,1,0:T(8,128)(2,1)S(1)}, u32[]{:S(2)}, u32[]{:S(2)}) collective-permute-start(bf16[1,128,128]{2,1,0:T(8,128)(2,1)S(1)} %shard_map.50), channel_id=1, source_target_pairs={{0,4},{1,5},{2,6},{3,7},{4,0},{5,1},{6,2},{7,3},{8,12},{9,13},{10,... | collective-permute-start | bytes 98312 | tf_op jit(solution)/shard_map/ppermute | solution.py:25
  19.4 4.0 %collective-permute-done.3.two_ref = bf16[1,128,128]{2,1,0:T(8,128)(2,1)S(1)} collective-permute-done((bf16[1,128,128]{2,1,0:T(8,128)(2,1)S(1)}, bf16[1,128,128]{2,1,0:T(8,128)(2,1)S(1)}, u32[]{:S(2)}, u32[]{:S(2)}) %collective-permute-start.3) | collective-permute-done | bytes 32800 | tf_op jit(solution)/shard_map/ppermute | solution.py:25
  23.5 21.1 %all_to_all.10.all_ref = bf16[4,128,128]{2,1,0:T(8,128)(2,1)S(1)} all-to-all(bf16[4,128,128]{2,1,0:T(8,128)(2,1)S(1)} %shard_map.52), channel_id=1, replica_groups={{0,8,16,24},{1,9,17,25},{2,10,18,26},{3,11,19,27},{4,12,20,28},{5,13,21..., dimensions={0} | all-to-all | bytes 262144 | tf_op jit(solution)/shard_map/all_to_all | solution.py:314
  44.6 0.9 shard_map.53
  45.4 6.8 %all-to-all-start.1 = ((bf16[16,128,128]{2,1,0:T(8,128)(2,1)}), bf16[16,128,128]{2,1,0:T(8,128)(2,1)S(1)}, u32[]{:S(2)}, u32[]{:S(2)}) async-start(bf16[16,128,128]{2,1,0:T(8,128)(2,1)} %get-tuple-element.16), calls=%async_computation.1 | async-start | bytes 1048576 | tf_op jit(solution)/shard_map/all_to_all | solution.py:317
  52.2 0.0 copy-start.1
  52.2 4.0 %collective-permute-start.5 = (bf16[2,128,128]{2,1,0:T(8,128)(2,1)S(1)}, bf16[2,128,128]{2,1,0:T(8,128)(2,1)S(1)}, u32[]{:S(2)}, u32[]{:S(2)}) collective-permute-start(bf16[2,128,128]{2,1,0:T(8,128)(2,1)S(1)} %get-tuple-element.15.refs_0_), channel_id=1, source_target_pairs={{0,4},{1,5},{2,6},{3,7},{4,0},{5,1},{6,2},{7,3},{8,12},{9,13},{10,... | collective-permute-start | bytes 196616 | tf_op jit(solution)/shard_map/ppermute | solution.py:25
  56.2 1.9 %collective-permute-start.2 = (bf16[2,128,128]{2,1,0:T(8,128)(2,1)S(1)}, bf16[2,128,128]{2,1,0:T(8,128)(2,1)S(1)}, u32[]{:S(2)}, u32[]{:S(2)}) collective-permute-start(bf16[2,128,128]{2,1,0:T(8,128)(2,1)S(1)} %get-tuple-element.14), channel_id=1, source_target_pairs={{0,2},{1,3},{2,0},{3,1},{4,6},{5,7},{6,4},{7,5},{8,10},{9,11},{10,... | collective-permute-start | bytes 196616 | tf_op jit(solution)/shard_map/ppermute | solution.py:25
  58.2 0.1 collective-permute-done.5.refs_1_
  58.3 3.5 %collective-permute-start.6 = (bf16[4,128,128]{2,1,0:T(8,128)(2,1)S(1)}, bf16[4,128,128]{2,1,0:T(8,128)(2,1)S(1)}, u32[]{:S(2)}, u32[]{:S(2)}) collective-permute-start(bf16[4,128,128]{2,1,0:T(8,128)(2,1)S(1)} %pad_maximum_fusion.1), channel_id=1, source_target_pairs={{0,2},{1,3},{2,0},{3,1},{4,6},{5,7},{6,4},{7,5},{8,10},{9,11},{10,... | collective-permute-start | bytes 393224 | tf_op jit(solution)/shard_map/ppermute | solution.py:25
  61.7 0.0 all-to-all-done.1.all_ref
  61.7 0.1 shard_map.54.refs_3_
  61.8 3.3 %collective-permute-start.7 = (bf16[4,128,128]{2,1,0:T(8,128)(2,1)S(1)}, bf16[4,128,128]{2,1,0:T(8,128)(2,1)S(1)}, u32[]{:S(2)}, u32[]{:S(2)}) collective-permute-start(bf16[4,128,128]{2,1,0:T(8,128)(2,1)S(1)} %shard_map.54.refs_3_), channel_id=1, source_target_pairs={{0,4},{1,5},{2,6},{3,7},{4,0},{5,1},{6,2},{7,3},{8,12},{9,13},{10,... | collective-permute-start | bytes 393224 | tf_op jit(solution)/shard_map/ppermute | solution.py:25
  65.2 0.0 collective-permute-done.2.other_ref
  65.2 2.8 %collective-permute-start.4 = (bf16[3,128,128]{2,1,0:T(8,128)(2,1)S(1)}, bf16[3,128,128]{2,1,0:T(8,128)(2,1)S(1)}, u32[]{:S(2)}, u32[]{:S(2)}) collective-permute-start(bf16[3,128,128]{2,1,0:T(8,128)(2,1)S(1)} %shard_map.51), channel_id=1, source_target_pairs={{0,4},{1,5},{2,6},{3,7},{4,0},{5,1},{6,2},{7,3},{8,12},{9,13},{10,... | collective-permute-start | bytes 294920 | tf_op jit(solution)/shard_map/ppermute | solution.py:25
  68.1 4.5 %collective-permute-done.4.rest_ref = bf16[3,128,128]{2,1,0:T(8,128)(2,1)S(1)} collective-permute-done((bf16[3,128,128]{2,1,0:T(8,128)(2,1)S(1)}, bf16[3,128,128]{2,1,0:T(8,128)(2,1)S(1)}, u32[]{:S(2)}, u32[]{:S(2)}) %collective-permute-start.4) | collective-permute-done | bytes 98336 | tf_op jit(solution)/shard_map/ppermute | solution.py:25
  72.5 0.0 collective-permute-done.6.refs_2_
  72.5 0.0 collective-permute-done.7.refs_4_
  72.6 0.1 shard_map.55.found_ref
  72.6 8.5 %collective-permute-start.8 = (bf16[28,128,128]{2,1,0:T(8,128)(2,1)S(1)}, bf16[28,128,128]{2,1,0:T(8,128)(2,1)S(1)}, u32[]{:S(2)}, u32[]{:S(2)}) collective-permute-start(bf16[28,128,128]{2,1,0:T(8,128)(2,1)S(1)} %shard_map.55.found_ref), channel_id=1, source_target_pairs={{0,1},{1,0},{2,3},{3,2},{4,5},{5,4},{6,7},{7,6},{8,9},{9,8},{10,11... | collective-permute-start | bytes 2752520 | tf_op jit(solution)/shard_map/ppermute | solution.py:25
  81.2 0.0 copy-start
  81.2 3.5 %collective-permute-start.9 = (bf16[8,128,128]{2,1,0:T(8,128)(2,1)S(1)}, bf16[8,128,128]{2,1,0:T(8,128)(2,1)S(1)}, u32[]{:S(2)}, u32[]{:S(2)}) collective-permute-start(bf16[8,128,128]{2,1,0:T(8,128)(2,1)S(1)} %pad_maximum_fusion), channel_id=1, source_target_pairs={{0,2},{1,3},{2,0},{3,1},{4,6},{5,7},{6,4},{7,5},{8,10},{9,11},{10,... | collective-permute-start | bytes 786440 | tf_op jit(solution)/shard_map/ppermute | solution.py:25
  84.7 6.4 %collective-permute-done.9.found_ref = bf16[8,128,128]{2,1,0:T(8,128)(2,1)S(1)} collective-permute-done((bf16[8,128,128]{2,1,0:T(8,128)(2,1)S(1)}, bf16[8,128,128]{2,1,0:T(8,128)(2,1)S(1)}, u32[]{:S(2)}, u32[]{:S(2)}) %collective-permute-start.9) | collective-permute-done | bytes 262176 | tf_op jit(solution)/shard_map/ppermute | solution.py:25
  91.1 2.8 %collective-permute-start.10 = (bf16[8,128,128]{2,1,0:T(8,128)(2,1)S(1)}, bf16[8,128,128]{2,1,0:T(8,128)(2,1)S(1)}, u32[]{:S(2)}, u32[]{:S(2)}) collective-permute-start(bf16[8,128,128]{2,1,0:T(8,128)(2,1)S(1)} %collective-permute-done.9.found_ref), channel_id=1, source_target_pairs={{0,1},{1,0},{2,3},{3,2},{4,5},{5,4},{6,7},{7,6},{8,9},{9,8},{10,11... | collective-permute-start | bytes 786440 | tf_op jit(solution)/shard_map/ppermute | solution.py:25
  93.9 0.0 copy-done.1
  93.9 5.8 %shard_map.46.a_hbm = f32[8,128,512]{2,1,0:T(8,128)} custom-call(bf16[512,1024]{1,0:T(8,128)(2,1)} %q_ref.7, bf16[512,1024]{1,0:T(8,128)(2,1)} %k_hbm.5, bf16[512,1024]{1,0:T(8,128)(2,1)} %v_hbm.5, f32[13,8,512]{2,1,0:T(8,128)S(1)} %copy-done.1), custom_call_target="tpu_custom_call" | custom-call | flops 1073741824 | bytes 3358720 | tf_op jit(solution)/shard_map/pallas_call | solution.py:49
  99.7 0.0 copy-done
  99.7 2.8 %shard_map.56 = (f32[2,128,512]{2,1,0:T(8,128)S(1)}, bf16[512,1024]{1,0:T(8,128)(2,1)}) custom-call(bf16[512,1024]{1,0:T(8,128)(2,1)S(1)} %copy-done, f32[8,128,512]{2,1,0:T(8,128)} %shard_map.46.a_hbm, f32[13,8,512]{2,1,0:T(8,128)S(1)} %copy-done.1, bf16[28,128,128]{2,1,0:T(8,128)(2,1)S(1)} %shard_map.55.found_ref), custom_call_target="tpu_custom_call" | custom-call | flops 469762048 | bytes 4276224 | tf_op jit(solution)/shard_map/pallas_call | solution.py:49
  102.5 0.0 collective-permute-done.8.found_ref
  102.5 2.8 %shard_map.57 = (f32[2,128,512]{2,1,0:T(8,128)S(1)}, bf16[512,1024]{1,0:T(8,128)(2,1)}) custom-call(bf16[512,1024]{1,0:T(8,128)(2,1)S(1)} %copy-done, f32[8,128,512]{2,1,0:T(8,128)} %shard_map.46.a_hbm, f32[13,8,512]{2,1,0:T(8,128)S(1)} %copy-done.1, bf16[28,128,128]{2,1,0:T(8,128)(2,1)S(1)} %collective-permute-done.8.found_ref, ...), custom_call_target="tpu_custom_call", output_to_operand_aliasing={{1}: (4, {})} | custom-call | flops 469762048 | bytes 5324800 | tf_op jit(solution)/shard_map/pallas_call | solution.py:49
  105.3 1.2 %shard_map.58.before_hbm = bf16[512,1024]{1,0:T(8,128)(2,1)} custom-call(bf16[512,1024]{1,0:T(8,128)(2,1)S(1)} %copy-done, f32[2,128,512]{2,1,0:T(8,128)S(1)} %get-tuple-element.19.t_ref, f32[13,8,512]{2,1,0:T(8,128)S(1)} %copy-done.1, bf16[8,128,128]{2,1,0:T(8,128)(2,1)S(1)} %collective-permute-done.9.found_ref, ...), custom_call_target="tpu_custom_call", output_to_operand_aliasing={{}: (4, {})} | custom-call | flops 134217728 | bytes 3096576 | tf_op jit(solution)/shard_map/pallas_call | solution.py:49
  106.5 0.0 collective-permute-done.10.found_ref
  106.6 1.2 %shard_map.59 = bf16[512,1024]{1,0:T(8,128)(2,1)} custom-call(bf16[512,1024]{1,0:T(8,128)(2,1)S(1)} %copy-done, f32[2,128,512]{2,1,0:T(8,128)S(1)} %get-tuple-element.18.t_ref, f32[13,8,512]{2,1,0:T(8,128)S(1)} %copy-done.1, bf16[8,128,128]{2,1,0:T(8,128)(2,1)S(1)} %collective-permute-done.10.found_ref, ...), custom_call_target="tpu_custom_call", output_to_operand_aliasing={{}: (4, {})} | custom-call | flops 134217728 | bytes 3096576 | tf_op jit(solution)/shard_map/pallas_call | solution.py:49
  (6 shorter events, 0.2 us)
Async XLA Ops:
  1.6 10.3 %collective-permute-start = (bf16[4,128,128]{2,1,0:T(8,128)(2,1)S(1)}, bf16[4,128,128]{2,1,0:T(8,128)(2,1)S(1)}, u32[]{:S(2)}, u32[]{:S(2)}) collective-permute-start(bf16[4,128,128]{2,1,0:T(8,128)(2,1)S(1)} %shard_map.48), channel_id=1, source_target_pairs={{0,1},{1,0},{2,3},{3,2},{4,5},{5,4},{6,7},{7,6},{8,9},{9,8},{10,11... | collective-permute-start | bytes 393224 | tf_op jit(solution)/shard_map/ppermute | solution.py:25
  12.0 5.5 %collective-permute-start.1 = (bf16[2,128,128]{2,1,0:T(8,128)(2,1)S(1)}, bf16[2,128,128]{2,1,0:T(8,128)(2,1)S(1)}, u32[]{:S(2)}, u32[]{:S(2)}) collective-permute-start(bf16[2,128,128]{2,1,0:T(8,128)(2,1)S(1)} %get-tuple-element.13), channel_id=1, source_target_pairs={{0,2},{1,3},{2,0},{3,1},{4,6},{5,7},{6,4},{7,5},{8,10},{9,11},{10,... | collective-permute-start | bytes 196616 | tf_op jit(solution)/shard_map/ppermute | solution.py:25
  17.5 5.9 %collective-permute-start.3 = (bf16[1,128,128]{2,1,0:T(8,128)(2,1)S(1)}, bf16[1,128,128]{2,1,0:T(8,128)(2,1)S(1)}, u32[]{:S(2)}, u32[]{:S(2)}) collective-permute-start(bf16[1,128,128]{2,1,0:T(8,128)(2,1)S(1)} %shard_map.50), channel_id=1, source_target_pairs={{0,4},{1,5},{2,6},{3,7},{4,0},{5,1},{6,2},{7,3},{8,12},{9,13},{10,... | collective-permute-start | bytes 98312 | tf_op jit(solution)/shard_map/ppermute | solution.py:25
  45.4 16.3 %all-to-all-start.1 = ((bf16[16,128,128]{2,1,0:T(8,128)(2,1)}), bf16[16,128,128]{2,1,0:T(8,128)(2,1)S(1)}, u32[]{:S(2)}, u32[]{:S(2)}) async-start(bf16[16,128,128]{2,1,0:T(8,128)(2,1)} %get-tuple-element.16), calls=%async_computation.1 | async-start | bytes 1048576 | tf_op jit(solution)/shard_map/all_to_all | solution.py:317
  52.2 41.7 %copy-start.1 = (f32[13,8,512]{2,1,0:T(8,128)S(1)}, f32[13,8,512]{2,1,0:T(8,128)}, u32[]{:S(2)}) copy-start(f32[13,8,512]{2,1,0:T(8,128)} %w_ref.9) | copy-start | bytes 638980
  52.2 6.0 %collective-permute-start.5 = (bf16[2,128,128]{2,1,0:T(8,128)(2,1)S(1)}, bf16[2,128,128]{2,1,0:T(8,128)(2,1)S(1)}, u32[]{:S(2)}, u32[]{:S(2)}) collective-permute-start(bf16[2,128,128]{2,1,0:T(8,128)(2,1)S(1)} %get-tuple-element.15.refs_0_), channel_id=1, source_target_pairs={{0,4},{1,5},{2,6},{3,7},{4,0},{5,1},{6,2},{7,3},{8,12},{9,13},{10,... | collective-permute-start | bytes 196616 | tf_op jit(solution)/shard_map/ppermute | solution.py:25
  56.2 8.9 %collective-permute-start.2 = (bf16[2,128,128]{2,1,0:T(8,128)(2,1)S(1)}, bf16[2,128,128]{2,1,0:T(8,128)(2,1)S(1)}, u32[]{:S(2)}, u32[]{:S(2)}) collective-permute-start(bf16[2,128,128]{2,1,0:T(8,128)(2,1)S(1)} %get-tuple-element.14), channel_id=1, source_target_pairs={{0,2},{1,3},{2,0},{3,1},{4,6},{5,7},{6,4},{7,5},{8,10},{9,11},{10,... | collective-permute-start | bytes 196616 | tf_op jit(solution)/shard_map/ppermute | solution.py:25
  58.3 14.3 %collective-permute-start.6 = (bf16[4,128,128]{2,1,0:T(8,128)(2,1)S(1)}, bf16[4,128,128]{2,1,0:T(8,128)(2,1)S(1)}, u32[]{:S(2)}, u32[]{:S(2)}) collective-permute-start(bf16[4,128,128]{2,1,0:T(8,128)(2,1)S(1)} %pad_maximum_fusion.1), channel_id=1, source_target_pairs={{0,2},{1,3},{2,0},{3,1},{4,6},{5,7},{6,4},{7,5},{8,10},{9,11},{10,... | collective-permute-start | bytes 393224 | tf_op jit(solution)/shard_map/ppermute | solution.py:25
  61.8 10.7 %collective-permute-start.7 = (bf16[4,128,128]{2,1,0:T(8,128)(2,1)S(1)}, bf16[4,128,128]{2,1,0:T(8,128)(2,1)S(1)}, u32[]{:S(2)}, u32[]{:S(2)}) collective-permute-start(bf16[4,128,128]{2,1,0:T(8,128)(2,1)S(1)} %shard_map.54.refs_3_), channel_id=1, source_target_pairs={{0,4},{1,5},{2,6},{3,7},{4,0},{5,1},{6,2},{7,3},{8,12},{9,13},{10,... | collective-permute-start | bytes 393224 | tf_op jit(solution)/shard_map/ppermute | solution.py:25
  65.2 7.3 %collective-permute-start.4 = (bf16[3,128,128]{2,1,0:T(8,128)(2,1)S(1)}, bf16[3,128,128]{2,1,0:T(8,128)(2,1)S(1)}, u32[]{:S(2)}, u32[]{:S(2)}) collective-permute-start(bf16[3,128,128]{2,1,0:T(8,128)(2,1)S(1)} %shard_map.51), channel_id=1, source_target_pairs={{0,4},{1,5},{2,6},{3,7},{4,0},{5,1},{6,2},{7,3},{8,12},{9,13},{10,... | collective-permute-start | bytes 294920 | tf_op jit(solution)/shard_map/ppermute | solution.py:25
  72.6 29.9 %collective-permute-start.8 = (bf16[28,128,128]{2,1,0:T(8,128)(2,1)S(1)}, bf16[28,128,128]{2,1,0:T(8,128)(2,1)S(1)}, u32[]{:S(2)}, u32[]{:S(2)}) collective-permute-start(bf16[28,128,128]{2,1,0:T(8,128)(2,1)S(1)} %shard_map.55.found_ref), channel_id=1, source_target_pairs={{0,1},{1,0},{2,3},{3,2},{4,5},{5,4},{6,7},{7,6},{8,9},{9,8},{10,11... | collective-permute-start | bytes 2752520 | tf_op jit(solution)/shard_map/ppermute | solution.py:25
  81.2 18.5 %copy-start = (bf16[512,1024]{1,0:T(8,128)(2,1)S(1)}, bf16[512,1024]{1,0:T(8,128)(2,1)}, u32[]{:S(2)}) copy-start(bf16[512,1024]{1,0:T(8,128)(2,1)} %q_ref.7) | copy-start | bytes 3145732
  81.2 9.9 %collective-permute-start.9 = (bf16[8,128,128]{2,1,0:T(8,128)(2,1)S(1)}, bf16[8,128,128]{2,1,0:T(8,128)(2,1)S(1)}, u32[]{:S(2)}, u32[]{:S(2)}) collective-permute-start(bf16[8,128,128]{2,1,0:T(8,128)(2,1)S(1)} %pad_maximum_fusion), channel_id=1, source_target_pairs={{0,2},{1,3},{2,0},{3,1},{4,6},{5,7},{6,4},{7,5},{8,10},{9,11},{10,... | collective-permute-start | bytes 786440 | tf_op jit(solution)/shard_map/ppermute | solution.py:25
  91.1 15.4 %collective-permute-start.10 = (bf16[8,128,128]{2,1,0:T(8,128)(2,1)S(1)}, bf16[8,128,128]{2,1,0:T(8,128)(2,1)S(1)}, u32[]{:S(2)}, u32[]{:S(2)}) collective-permute-start(bf16[8,128,128]{2,1,0:T(8,128)(2,1)S(1)} %collective-permute-done.9.found_ref), channel_id=1, source_target_pairs={{0,1},{1,0},{2,3},{3,2},{4,5},{5,4},{6,7},{7,6},{8,9},{9,8},{10,11... | collective-permute-start | bytes 786440 | tf_op jit(solution)/shard_map/ppermute | solution.py:25

commit v2 on v1

--- a/solution.py
+++ b/solution.py
@@ -62,67 +62,70 @@
     return pl.ds(start if isinstance(start, int) else pl.multiple_of(start, DK), DK)
 
 
-def state_kernel(flip, k_hbm, v_hbm, o_ref, k_ref, v_ref, sems):
-    width = k_ref.shape[1]
-    at = pl.ds(pl.multiple_of((my_place()[1] ^ flip) * width, width), width)
-    copies = [
-        pltpu.make_async_copy(src.at[:, at], dst, sems.at[i])
-        for i, (src, dst) in enumerate(((k_hbm, k_ref), (v_hbm, v_ref)))
-    ]
-    for copy in copies:
-        copy.start()
-    for copy in copies:
-        copy.wait()
+def fetch(pairs, side, sems):
+    copies = []
+    for i, (src, dst) in enumerate(pairs):
+        width = dst.shape[1]
+        at = pl.ds(pl.multiple_of(side * width, width), width)
+        copies.append(pltpu.make_async_copy(src.at[:, at], dst, sems.at[i]))
+        copies[-1].start()
+    return copies
+
+
+def put_states(k_ref, v_ref, o_ref):
     for n in range(o_ref.shape[0]):
         o_ref[n] = lax.dot_general(
             v_ref[:, lanes(n)], k_ref[:, lanes(n)], (((0,), (0,)), ((), ())), preferred_element_type=F32
         ).astype(BF16)
 
 
-def half_states(flip, keys, values):
+def send_kernel(k_hbm, v_hbm, o_ref, own_k_ref, own_v_ref, k_ref, v_ref, sems, own_sems):
+    copies = fetch(((k_hbm, k_ref), (v_hbm, v_ref)), 1 - my_place()[1], sems)
+    own = fetch(((k_hbm, own_k_ref), (v_hbm, own_v_ref)), my_place()[1], own_sems)
+    for copy in copies:
+        copy.wait()
+    put_states(k_ref, v_ref, o_ref)
+    for copy in own:
+        copy.wait()
+
+
+def send_states(keys, values):
     rows, width = keys.shape
-    buffer = pltpu.VMEM((rows, width // 2), BF16)
+    half = jax.ShapeDtypeStruct((rows, width // 2), BF16)
+    buffer = pltpu.VMEM(half.shape, BF16)
+    two = pltpu.SemaphoreType.DMA((2,))
     return kernel_call(
-        functools.partial(state_kernel, flip),
-        states(width // DK // 2),
+        send_kernel,
+        [states(width // DK // 2), half, half],
         [in_hbm(keys), in_hbm(values)],
         flops=rows * DK * width,
         spaces=[HBM, HBM],
-        scratch_shapes=[buffer, buffer, pltpu.SemaphoreType.DMA((2,))],
+        scratch_shapes=[buffer, buffer, two, two],
     )
 
 
-def local_kernel(q_hbm, k_hbm, v_hbm, w_ref, o_hbm, q_ref, k_ref, v_ref, o_ref, sems, out_sems):
-    rows, width = q_ref.shape
-    heads = o_ref.shape[0]
-    copies = []
-    for part in range(2):
-        at = pl.ds(part * width // 2, width // 2)
-        pairs = ((q_hbm, q_ref), (k_hbm, k_ref), (v_hbm, v_ref))
-        copies.append(
-            [pltpu.make_async_copy(x.at[:, at], y.at[:, at], sems.at[part, i]) for i, (x, y) in enumerate(pairs)]
-        )
-    for copy in copies[0] + copies[1]:
-        copy.start()
+def local_kernel(other, q_hbm, k_hbm, v_hbm, w_ref, o_ref, q_ref, k_ref, v_ref, sems):
+    side = my_place()[1] ^ other
+    copies = fetch(((q_hbm, q_ref), (k_hbm, k_ref), (v_hbm, v_ref)), side, sems)
+    rows = q_ref.shape[0]
+    half = o_ref.shape[0]
     tile = 2 * STRETCH
     key = lax.broadcasted_iota(jnp.int32, (tile, tile), 0)
     tok = lax.broadcasted_iota(jnp.int32, (tile, tile), 1)
     low = jnp.logical_and(tok >= STRETCH, key < STRETCH)
     same = jnp.logical_and(key <= tok, jnp.logical_not(low))
-    results = []
-    for head in range(heads):
-        if head % (heads // 2) == 0:
-            for copy in copies[head // (heads // 2)]:
-                copy.wait()
-        at = lanes(head)
+    for copy in copies:
+        copy.wait()
+    for n in range(half):
+        at = lanes(n)
+        head = side * half + n
         value_t = v_ref[:, at].T
+        levels = 1 + (rows // STRETCH).bit_length() - 1
+        scales = [w_ref[level, pl.ds(head, 1), :] * level_factor(level) for level in range(levels)]
         for r in range(rows // tile):
             here = pl.ds(r * tile, tile)
             span = (r + 1) * tile
-
-            def scale(level):
-                return w_ref[level, pl.ds(head, 1), here] * level_factor(level)
-
+            scale = lambda level: scales[level][:, r * tile : (r + 1) * tile]
             score = lax.dot_general(
                 k_ref[pl.ds(0, span), at], q_ref[here, at], (((1,), (1,)), ((), ())),
                 preferred_element_type=F32,
@@ -133,33 +136,19 @@
             weight = jnp.where(same, scale(0), jnp.where(low, scale(1), 0.0))
             parts.append(score[r * tile :] * weight)
             weighted = jnp.concatenate([p.astype(BF16) for p in parts], axis=0)
-            o_ref[head, :, here] = jnp.dot(value_t[:, :span], weighted, preferred_element_type=F32)
-        results.append(pltpu.make_async_copy(o_ref.at[head], o_hbm.at[head], out_sems.at[head]))
-        results[-1].start()
-    for copy in results:
-        copy.wait()
-
-
-def local_part(queries, keys, values, weights):
+            o_ref[n, :, here] = jnp.dot(value_t[:, :span], weighted, preferred_element_type=F32)
+
+
+def local_part(other, queries, keys, values, weights):
     rows, width = queries.shape
-    buffer = pltpu.VMEM((rows, width), BF16)
-    heads = width // DK
+    buffer = pltpu.VMEM((rows, width // 2), BF16)
     return kernel_call(
-        local_kernel,
-        pltpu.HBM((heads, DK, rows), F32),
+        functools.partial(local_kernel, other),
+        jax.ShapeDtypeStruct((width // DK // 2, DK, rows), F32),
         [in_hbm(queries), in_hbm(keys), in_hbm(values), weights],
-        limit=32,
-        flops=4 * rows * rows * width,
+        flops=2 * rows * rows * width,
         spaces=[HBM, HBM, HBM, VMEM],
-        out_specs=HBM,
-        scratch_shapes=[
-            buffer,
-            buffer,
-            buffer,
-            pltpu.VMEM((heads, DK, rows), F32),
-            pltpu.SemaphoreType.DMA((2, 3)),
-            pltpu.SemaphoreType.DMA((heads,)),
-        ],
+        scratch_shapes=[buffer, buffer, buffer, pltpu.SemaphoreType.DMA((3,))],
     )
 
 
@@ -248,19 +237,13 @@
     copies[-1].start()
 
 
-def near_kernel(other, mid, late, local_bits, q_ref, a_hbm, w_ref, found_ref, *refs):
-    t_ref, out_hbm, o_ref, sems, a_ref, a_sems = refs[-6:]
+def near_kernel(other, mid, late, local_bits, q_ref, a_ref, w_ref, found_ref, *refs):
+    t_ref, out_hbm, o_ref, sems = refs[-4:]
     half = a_ref.shape[0]
-    locals_ = []
-    for slot in range(half):
-        head = (my_place()[1] ^ other) * half + slot_head(slot)
-        locals_.append(pltpu.make_async_copy(a_hbm.at[head], a_ref.at[slot], a_sems.at[slot]))
-        locals_[-1].start()
     copies = []
     for slot in range(half):
         n = slot_head(slot)
         head = (my_place()[1] ^ other) * half + n
-        locals_[slot].wait()
         found = [found_ref[level * half + n] for level in range(3)]
         found.append(found_ref[pl.ds(3 * half + slot * mid, mid)].reshape(mid * DK, DK))
         bits = 3 + mid
@@ -268,7 +251,7 @@
             found.append(found_ref[pl.ds((3 + mid) * half + slot * late, late)].reshape(late * DK, DK))
             bits += late
         found = jnp.concatenate(found, axis=0)
-        total = add_levels(q_ref, w_ref, a_ref[slot], head, found, range(bits), local_bits)
+        total = add_levels(q_ref, w_ref, a_ref[n], head, found, range(bits), local_bits)
         if slot < 2:
             send_out(o_ref, sems, out_hbm, copies, total, head)
         else:
@@ -298,9 +281,9 @@
     blocks = lax.axis_size("ctx")
     runs = lax.axis_size("grp")
     groups = blocks // 8
-    send = half_states(1, keys, values)
+    send, own_keys, own_values = send_states(keys, values)
     first = swap(send, "ctx", 1)
-    keep = half_states(0, keys, values)
+    keep = kernel_call(put_states, states(half), [own_keys, own_values], flops=rows * DK * width)
     pair, pair_rest = kernel_call(pair_kernel, [states(2), states(half - 2)], [keep, first])
     one_z = swap(pair, "ctx", 2)
     one_rest = swap(pair_rest, "ctx", 2)
@@ -308,7 +291,7 @@
     two_z = swap(ahead, "ctx", 4)
     rest = kernel_call(rest_kernel, states(half - 1), [keep, first, one_z, one_rest])
     two_rest = swap(rest, "ctx", 4)
-    local = local_part(queries, keys, values, level_weights)
+    locals_ = [local_part(other, queries, keys, values, level_weights) for other in (0, 1)]
     picked = kernel_call(pick_kernel, states(groups), [keep, first, one_z, two_z])
     members = [[low + 8 * g for g in range(groups)] for low in range(8)]
     group_sums = lax.all_to_all(picked, "ctx", 0, 0, axis_index_groups=members, tiled=True)
@@ -336,12 +319,12 @@
         return kernel_call(
             functools.partial(near_kernel, other, mid, late, local_bits),
             [jax.ShapeDtypeStruct((half - 2, DK, rows), F32), out_type],
-            [queries, in_hbm(local), level_weights, found, *before],
+            [queries, locals_[other], level_weights, found, *before],
             limit=24,
             flops=2 * rows * DK * DK * (half * (3 + mid) + 2 * late),
-            spaces=[VMEM, HBM, VMEM, VMEM] + [HBM] * len(before),
+            spaces=[VMEM] * 4 + [HBM] * len(before),
             out_specs=[VMEM, HBM],
-            scratch_shapes=out_buffers(2) + [pltpu.VMEM((half, DK, rows), F32), pltpu.SemaphoreType.DMA((half,))],
+            scratch_shapes=out_buffers(2),
             input_output_aliases={4: 1} if before else {},
         )
 

time: 108 us -> 107 us (level)
  Pallas kernels: 18.1 us -> 15.8 us
  waiting for transfers between devices: 18.5 us -> 20 us
    pallas_call x14 -> x15, Pallas kernels: 18.1 us -> 15.8 us  [kernel_call(): pl.pallas_call(kernel, out_shape=outs, in_specs=spaces or [VMEM] * len(op...]
    ppermute x11, waiting for transfers between devices: 18.5 us -> 20 us  [swap(): return lax.ppermute(block, axis, [(i, i ^ stride) for i in range(count)])]
  transfers between devices with their start and end apart: 12 -> 12, of which waited for: 5 -> 5; matrix products, arithmetic and copies ran while one was open for 0% -> 0% of each run, Pallas kernels for 13% -> 11%
where the time goes in v2:
time: 107 us
  starting transfers between devices  49.4 us (46%)
  blocking collectives  21.1 us (20%)
  waiting for transfers between devices  20 us (19%)
  Pallas kernels  15.8 us (15%)
    ppermute x11, starting transfers between devices, swap(): return lax.ppermute(block, axis, [(i, i ^ stride) for i in range(count)])  42.7 us
    all_to_all x1, blocking collectives, attend(): lax.all_to_all(picked, 'ctx', 0, 0, axis_index_groups=members, tiled=True)  21.1 us
    ppermute x11, waiting for transfers between devices, swap(): return lax.ppermute(block, axis, [(i, i ^ stride) for i in range(count)])  20 us
    pallas_call x15, Pallas kernels, kernel_call(): pl.pallas_call(kernel, out_shape=outs, in_specs=spaces or [VMEM] * len(op...  15.8 us
    all_to_all x1, starting transfers between devices, attend(): run_states = lax.all_to_all(spread, 'grp', 0, 0, tiled=True)  6.76 us
  transfers between devices with their start and end apart: 12, of which 5 were waited for; matrix products, arithmetic and copies ran while one was open for 0% of the time, Pallas kernels for 11%

profile of v2, /device:TPU:1, one launch (start us, length us, event | category | flops | bytes accessed | tf_op | source)
XLA Modules:
  0.0 106.7 jit_solution(4001705722913256811)
XLA Ops:
  0.0 1.7 %shard_map.47 = (bf16[4,128,128]{2,1,0:T(8,128)(2,1)S(1)}, bf16[512,512]{1,0:T(8,128)(2,1)S(1)}, bf16[512,512]{1,0:T(8,128)(2,1)S(1)}) custom-call(bf16[512,1024]{1,0:T(8,128)(2,1)} %k_hbm.5, bf16[512,1024]{1,0:T(8,128)(2,1)} %v_hbm.5), custom_call_target="tpu_custom_call" | custom-call | flops 67108864 | bytes 2097152 | tf_op jit(solution)/shard_map/pallas_call | solution.py:49
  1.8 8.7 %collective-permute-start = (bf16[4,128,128]{2,1,0:T(8,128)(2,1)S(1)}, bf16[4,128,128]{2,1,0:T(8,128)(2,1)S(1)}, u32[]{:S(2)}, u32[]{:S(2)}) collective-permute-start(bf16[4,128,128]{2,1,0:T(8,128)(2,1)S(1)} %get-tuple-element.18), channel_id=1, source_target_pairs={{0,1},{1,0},{2,3},{3,2},{4,5},{5,4},{6,7},{7,6},{8,9},{9,8},{10,11... | collective-permute-start | bytes 393224 | tf_op jit(solution)/shard_map/ppermute | solution.py:25
  10.5 0.3 shard_map.48.keep_ref
  10.9 0.6 collective-permute-done.first_ref
  11.5 1.9 %collective-permute-start.1 = (bf16[2,128,128]{2,1,0:T(8,128)(2,1)S(1)}, bf16[2,128,128]{2,1,0:T(8,128)(2,1)S(1)}, u32[]{:S(2)}, u32[]{:S(2)}) collective-permute-start(bf16[2,128,128]{2,1,0:T(8,128)(2,1)S(1)} %get-tuple-element.19), channel_id=1, source_target_pairs={{0,2},{1,3},{2,0},{3,1},{4,6},{5,7},{6,4},{7,5},{8,10},{9,11},{10,... | collective-permute-start | bytes 196616 | tf_op jit(solution)/shard_map/ppermute | solution.py:25
  13.4 3.1 %collective-permute-done.1.one_ref = bf16[2,128,128]{2,1,0:T(8,128)(2,1)S(1)} collective-permute-done((bf16[2,128,128]{2,1,0:T(8,128)(2,1)S(1)}, bf16[2,128,128]{2,1,0:T(8,128)(2,1)S(1)}, u32[]{:S(2)}, u32[]{:S(2)}) %collective-permute-start.1) | collective-permute-done | bytes 65568 | tf_op jit(solution)/shard_map/ppermute | solution.py:25
  16.5 1.9 %collective-permute-start.3 = (bf16[1,128,128]{2,1,0:T(8,128)(2,1)S(1)}, bf16[1,128,128]{2,1,0:T(8,128)(2,1)S(1)}, u32[]{:S(2)}, u32[]{:S(2)}) collective-permute-start(bf16[1,128,128]{2,1,0:T(8,128)(2,1)S(1)} %shard_map.50), channel_id=1, source_target_pairs={{0,4},{1,5},{2,6},{3,7},{4,0},{5,1},{6,2},{7,3},{8,12},{9,13},{10,... | collective-permute-start | bytes 98312 | tf_op jit(solution)/shard_map/ppermute | solution.py:25
  18.5 4.0 %collective-permute-done.3.two_ref = bf16[1,128,128]{2,1,0:T(8,128)(2,1)S(1)} collective-permute-done((bf16[1,128,128]{2,1,0:T(8,128)(2,1)S(1)}, bf16[1,128,128]{2,1,0:T(8,128)(2,1)S(1)}, u32[]{:S(2)}, u32[]{:S(2)}) %collective-permute-start.3) | collective-permute-done | bytes 32800 | tf_op jit(solution)/shard_map/ppermute | solution.py:25
  22.5 21.1 %all_to_all.10.all_ref = bf16[4,128,128]{2,1,0:T(8,128)(2,1)S(1)} all-to-all(bf16[4,128,128]{2,1,0:T(8,128)(2,1)S(1)} %shard_map.52), channel_id=1, replica_groups={{0,8,16,24},{1,9,17,25},{2,10,18,26},{3,11,19,27},{4,12,20,28},{5,13,21..., dimensions={0} | all-to-all | bytes 262144 | tf_op jit(solution)/shard_map/all_to_all | solution.py:297
  43.6 0.9 shard_map.53
  44.4 6.8 %all-to-all-start.1 = ((bf16[16,128,128]{2,1,0:T(8,128)(2,1)}), bf16[16,128,128]{2,1,0:T(8,128)(2,1)S(1)}, u32[]{:S(2)}, u32[]{:S(2)}) async-start(bf16[16,128,128]{2,1,0:T(8,128)(2,1)} %get-tuple-element.22), calls=%async_computation.1 | async-start | bytes 1048576 | tf_op jit(solution)/shard_map/all_to_all | solution.py:300
  51.2 4.3 %collective-permute-start.5 = (bf16[2,128,128]{2,1,0:T(8,128)(2,1)S(1)}, bf16[2,128,128]{2,1,0:T(8,128)(2,1)S(1)}, u32[]{:S(2)}, u32[]{:S(2)}) collective-permute-start(bf16[2,128,128]{2,1,0:T(8,128)(2,1)S(1)} %get-tuple-element.21.refs_0_), channel_id=1, source_target_pairs={{0,4},{1,5},{2,6},{3,7},{4,0},{5,1},{6,2},{7,3},{8,12},{9,13},{10,... | collective-permute-start | bytes 196616 | tf_op jit(solution)/shard_map/ppermute | solution.py:25
  55.6 1.9 %collective-permute-start.2 = (bf16[2,128,128]{2,1,0:T(8,128)(2,1)S(1)}, bf16[2,128,128]{2,1,0:T(8,128)(2,1)S(1)}, u32[]{:S(2)}, u32[]{:S(2)}) collective-permute-start(bf16[2,128,128]{2,1,0:T(8,128)(2,1)S(1)} %get-tuple-element.20), channel_id=1, source_target_pairs={{0,2},{1,3},{2,0},{3,1},{4,6},{5,7},{6,4},{7,5},{8,10},{9,11},{10,... | collective-permute-start | bytes 196616 | tf_op jit(solution)/shard_map/ppermute | solution.py:25
  57.5 0.0 collective-permute-done.5.refs_1_
  57.5 3.4 %collective-permute-start.6 = (bf16[4,128,128]{2,1,0:T(8,128)(2,1)S(1)}, bf16[4,128,128]{2,1,0:T(8,128)(2,1)S(1)}, u32[]{:S(2)}, u32[]{:S(2)}) collective-permute-start(bf16[4,128,128]{2,1,0:T(8,128)(2,1)S(1)} %pad_maximum_fusion.1), channel_id=1, source_target_pairs={{0,2},{1,3},{2,0},{3,1},{4,6},{5,7},{6,4},{7,5},{8,10},{9,11},{10,... | collective-permute-start | bytes 393224 | tf_op jit(solution)/shard_map/ppermute | solution.py:25
  60.9 0.0 all-to-all-done.1.all_ref
  60.9 0.1 shard_map.54.refs_3_
  61.0 3.6 %collective-permute-start.7 = (bf16[4,128,128]{2,1,0:T(8,128)(2,1)S(1)}, bf16[4,128,128]{2,1,0:T(8,128)(2,1)S(1)}, u32[]{:S(2)}, u32[]{:S(2)}) collective-permute-start(bf16[4,128,128]{2,1,0:T(8,128)(2,1)S(1)} %shard_map.54.refs_3_), channel_id=1, source_target_pairs={{0,4},{1,5},{2,6},{3,7},{4,0},{5,1},{6,2},{7,3},{8,12},{9,13},{10,... | collective-permute-start | bytes 393224 | tf_op jit(solution)/shard_map/ppermute | solution.py:25
  64.6 0.0 collective-permute-done.2.other_ref
  64.7 2.6 %collective-permute-start.4 = (bf16[3,128,128]{2,1,0:T(8,128)(2,1)S(1)}, bf16[3,128,128]{2,1,0:T(8,128)(2,1)S(1)}, u32[]{:S(2)}, u32[]{:S(2)}) collective-permute-start(bf16[3,128,128]{2,1,0:T(8,128)(2,1)S(1)} %shard_map.51), channel_id=1, source_target_pairs={{0,4},{1,5},{2,6},{3,7},{4,0},{5,1},{6,2},{7,3},{8,12},{9,13},{10,... | collective-permute-start | bytes 294920 | tf_op jit(solution)/shard_map/ppermute | solution.py:25
  67.2 4.8 %collective-permute-done.4.rest_ref = bf16[3,128,128]{2,1,0:T(8,128)(2,1)S(1)} collective-permute-done((bf16[3,128,128]{2,1,0:T(8,128)(2,1)S(1)}, bf16[3,128,128]{2,1,0:T(8,128)(2,1)S(1)}, u32[]{:S(2)}, u32[]{:S(2)}) %collective-permute-start.4) | collective-permute-done | bytes 98336 | tf_op jit(solution)/shard_map/ppermute | solution.py:25
  72.0 0.0 collective-permute-done.6.refs_2_
  72.0 0.0 collective-permute-done.7.refs_4_
  72.0 0.1 shard_map.55.found_ref
  72.1 0.0 copy-start.1
  72.1 9.3 %collective-permute-start.8 = (bf16[28,128,128]{2,1,0:T(8,128)(2,1)S(1)}, bf16[28,128,128]{2,1,0:T(8,128)(2,1)S(1)}, u32[]{:S(2)}, u32[]{:S(2)}) collective-permute-start(bf16[28,128,128]{2,1,0:T(8,128)(2,1)S(1)} %shard_map.55.found_ref), channel_id=1, source_target_pairs={{0,1},{1,0},{2,3},{3,2},{4,5},{5,4},{6,7},{7,6},{8,9},{9,8},{10,11... | collective-permute-start | bytes 2752520 | tf_op jit(solution)/shard_map/ppermute | solution.py:25
  81.5 2.1 %collective-permute-start.9 = (bf16[8,128,128]{2,1,0:T(8,128)(2,1)S(1)}, bf16[8,128,128]{2,1,0:T(8,128)(2,1)S(1)}, u32[]{:S(2)}, u32[]{:S(2)}) collective-permute-start(bf16[8,128,128]{2,1,0:T(8,128)(2,1)S(1)} %pad_maximum_fusion), channel_id=1, source_target_pairs={{0,2},{1,3},{2,0},{3,1},{4,6},{5,7},{6,4},{7,5},{8,10},{9,11},{10,... | collective-permute-start | bytes 786440 | tf_op jit(solution)/shard_map/ppermute | solution.py:25
  83.6 7.6 %collective-permute-done.9.found_ref = bf16[8,128,128]{2,1,0:T(8,128)(2,1)S(1)} collective-permute-done((bf16[8,128,128]{2,1,0:T(8,128)(2,1)S(1)}, bf16[8,128,128]{2,1,0:T(8,128)(2,1)S(1)}, u32[]{:S(2)}, u32[]{:S(2)}) %collective-permute-start.9) | collective-permute-done | bytes 262176 | tf_op jit(solution)/shard_map/ppermute | solution.py:25
  91.2 2.8 %collective-permute-start.10 = (bf16[8,128,128]{2,1,0:T(8,128)(2,1)S(1)}, bf16[8,128,128]{2,1,0:T(8,128)(2,1)S(1)}, u32[]{:S(2)}, u32[]{:S(2)}) collective-permute-start(bf16[8,128,128]{2,1,0:T(8,128)(2,1)S(1)} %collective-permute-done.9.found_ref), channel_id=1, source_target_pairs={{0,1},{1,0},{2,3},{3,2},{4,5},{5,4},{6,7},{7,6},{8,9},{9,8},{10,11... | collective-permute-start | bytes 786440 | tf_op jit(solution)/shard_map/ppermute | solution.py:25
  94.0 0.0 copy-done.1
  94.0 3.3 %shard_map.56.a_ref = f32[4,128,512]{2,1,0:T(8,128)S(1)} custom-call(bf16[512,1024]{1,0:T(8,128)(2,1)} %q_ref.7, bf16[512,1024]{1,0:T(8,128)(2,1)} %k_hbm.5, bf16[512,1024]{1,0:T(8,128)(2,1)} %v_hbm.5, f32[13,8,512]{2,1,0:T(8,128)S(1)} %copy-done.1), custom_call_target="tpu_custom_call" | custom-call | flops 536870912 | bytes 3358720 | tf_op jit(solution)/shard_map/pallas_call | solution.py:49
  97.3 0.0 copy-start
  97.3 3.3 %shard_map.46.a_ref = f32[4,128,512]{2,1,0:T(8,128)S(1)} custom-call(bf16[512,1024]{1,0:T(8,128)(2,1)} %q_ref.7, bf16[512,1024]{1,0:T(8,128)(2,1)} %k_hbm.5, bf16[512,1024]{1,0:T(8,128)(2,1)} %v_hbm.5, f32[13,8,512]{2,1,0:T(8,128)S(1)} %copy-done.1), custom_call_target="tpu_custom_call" | custom-call | flops 536870912 | bytes 3358720 | tf_op jit(solution)/shard_map/pallas_call | solution.py:49
  100.6 0.0 copy-done
  100.7 1.8 %shard_map.57 = (f32[2,128,512]{2,1,0:T(8,128)S(1)}, bf16[512,1024]{1,0:T(8,128)(2,1)}) custom-call(bf16[512,1024]{1,0:T(8,128)(2,1)S(1)} %copy-done, f32[4,128,512]{2,1,0:T(8,128)S(1)} %shard_map.56.a_ref, f32[13,8,512]{2,1,0:T(8,128)S(1)} %copy-done.1, bf16[28,128,128]{2,1,0:T(8,128)(2,1)S(1)} %shard_map.55.found_ref), custom_call_target="tpu_custom_call" | custom-call | flops 469762048 | bytes 3227648 | tf_op jit(solution)/shard_map/pallas_call | solution.py:49
  102.4 0.0 collective-permute-done.8.found_ref
  102.4 1.8 %shard_map.58 = (f32[2,128,512]{2,1,0:T(8,128)S(1)}, bf16[512,1024]{1,0:T(8,128)(2,1)}) custom-call(bf16[512,1024]{1,0:T(8,128)(2,1)S(1)} %copy-done, f32[4,128,512]{2,1,0:T(8,128)S(1)} %shard_map.46.a_ref, f32[13,8,512]{2,1,0:T(8,128)S(1)} %copy-done.1, bf16[28,128,128]{2,1,0:T(8,128)(2,1)S(1)} %collective-permute-done.8.found_ref, ...), custom_call_target="tpu_custom_call", output_to_operand_aliasing={{1}: (4, {})} | custom-call | flops 469762048 | bytes 4276224 | tf_op jit(solution)/shard_map/pallas_call | solution.py:49
  104.3 1.2 %shard_map.59.before_hbm = bf16[512,1024]{1,0:T(8,128)(2,1)} custom-call(bf16[512,1024]{1,0:T(8,128)(2,1)S(1)} %copy-done, f32[2,128,512]{2,1,0:T(8,128)S(1)} %get-tuple-element.25.t_ref, f32[13,8,512]{2,1,0:T(8,128)S(1)} %copy-done.1, bf16[8,128,128]{2,1,0:T(8,128)(2,1)S(1)} %collective-permute-done.9.found_ref, ...), custom_call_target="tpu_custom_call", output_to_operand_aliasing={{}: (4, {})} | custom-call | flops 134217728 | bytes 3096576 | tf_op jit(solution)/shard_map/pallas_call | solution.py:49
  105.5 0.0 collective-permute-done.10.found_ref
  105.5 1.2 %shard_map.60 = bf16[512,1024]{1,0:T(8,128)(2,1)} custom-call(bf16[512,1024]{1,0:T(8,128)(2,1)S(1)} %copy-done, f32[2,128,512]{2,1,0:T(8,128)S(1)} %get-tuple-element.24.t_ref, f32[13,8,512]{2,1,0:T(8,128)S(1)} %copy-done.1, bf16[8,128,128]{2,1,0:T(8,128)(2,1)S(1)} %collective-permute-done.10.found_ref, ...), custom_call_target="tpu_custom_call", output_to_operand_aliasing={{}: (4, {})} | custom-call | flops 134217728 | bytes 3096576 | tf_op jit(solution)/shard_map/pallas_call | solution.py:49
  (6 shorter events, 0.2 us)
Async XLA Ops:
  1.8 9.7 %collective-permute-start = (bf16[4,128,128]{2,1,0:T(8,128)(2,1)S(1)}, bf16[4,128,128]{2,1,0:T(8,128)(2,1)S(1)}, u32[]{:S(2)}, u32[]{:S(2)}) collective-permute-start(bf16[4,128,128]{2,1,0:T(8,128)(2,1)S(1)} %get-tuple-element.18), channel_id=1, source_target_pairs={{0,1},{1,0},{2,3},{3,2},{4,5},{5,4},{6,7},{7,6},{8,9},{9,8},{10,11... | collective-permute-start | bytes 393224 | tf_op jit(solution)/shard_map/ppermute | solution.py:25
  11.5 5.0 %collective-permute-start.1 = (bf16[2,128,128]{2,1,0:T(8,128)(2,1)S(1)}, bf16[2,128,128]{2,1,0:T(8,128)(2,1)S(1)}, u32[]{:S(2)}, u32[]{:S(2)}) collective-permute-start(bf16[2,128,128]{2,1,0:T(8,128)(2,1)S(1)} %get-tuple-element.19), channel_id=1, source_target_pairs={{0,2},{1,3},{2,0},{3,1},{4,6},{5,7},{6,4},{7,5},{8,10},{9,11},{10,... | collective-permute-start | bytes 196616 | tf_op jit(solution)/shard_map/ppermute | solution.py:25
  16.5 5.9 %collective-permute-start.3 = (bf16[1,128,128]{2,1,0:T(8,128)(2,1)S(1)}, bf16[1,128,128]{2,1,0:T(8,128)(2,1)S(1)}, u32[]{:S(2)}, u32[]{:S(2)}) collective-permute-start(bf16[1,128,128]{2,1,0:T(8,128)(2,1)S(1)} %shard_map.50), channel_id=1, source_target_pairs={{0,4},{1,5},{2,6},{3,7},{4,0},{5,1},{6,2},{7,3},{8,12},{9,13},{10,... | collective-permute-start | bytes 98312 | tf_op jit(solution)/shard_map/ppermute | solution.py:25
  44.4 16.5 %all-to-all-start.1 = ((bf16[16,128,128]{2,1,0:T(8,128)(2,1)}), bf16[16,128,128]{2,1,0:T(8,128)(2,1)S(1)}, u32[]{:S(2)}, u32[]{:S(2)}) async-start(bf16[16,128,128]{2,1,0:T(8,128)(2,1)} %get-tuple-element.22), calls=%async_computation.1 | async-start | bytes 1048576 | tf_op jit(solution)/shard_map/all_to_all | solution.py:300
  51.2 6.3 %collective-permute-start.5 = (bf16[2,128,128]{2,1,0:T(8,128)(2,1)S(1)}, bf16[2,128,128]{2,1,0:T(8,128)(2,1)S(1)}, u32[]{:S(2)}, u32[]{:S(2)}) collective-permute-start(bf16[2,128,128]{2,1,0:T(8,128)(2,1)S(1)} %get-tuple-element.21.refs_0_), channel_id=1, source_target_pairs={{0,4},{1,5},{2,6},{3,7},{4,0},{5,1},{6,2},{7,3},{8,12},{9,13},{10,... | collective-permute-start | bytes 196616 | tf_op jit(solution)/shard_map/ppermute | solution.py:25
  55.6 9.1 %collective-permute-start.2 = (bf16[2,128,128]{2,1,0:T(8,128)(2,1)S(1)}, bf16[2,128,128]{2,1,0:T(8,128)(2,1)S(1)}, u32[]{:S(2)}, u32[]{:S(2)}) collective-permute-start(bf16[2,128,128]{2,1,0:T(8,128)(2,1)S(1)} %get-tuple-element.20), channel_id=1, source_target_pairs={{0,2},{1,3},{2,0},{3,1},{4,6},{5,7},{6,4},{7,5},{8,10},{9,11},{10,... | collective-permute-start | bytes 196616 | tf_op jit(solution)/shard_map/ppermute | solution.py:25
  57.5 14.5 %collective-permute-start.6 = (bf16[4,128,128]{2,1,0:T(8,128)(2,1)S(1)}, bf16[4,128,128]{2,1,0:T(8,128)(2,1)S(1)}, u32[]{:S(2)}, u32[]{:S(2)}) collective-permute-start(bf16[4,128,128]{2,1,0:T(8,128)(2,1)S(1)} %pad_maximum_fusion.1), channel_id=1, source_target_pairs={{0,2},{1,3},{2,0},{3,1},{4,6},{5,7},{6,4},{7,5},{8,10},{9,11},{10,... | collective-permute-start | bytes 393224 | tf_op jit(solution)/shard_map/ppermute | solution.py:25
  61.0 11.0 %collective-permute-start.7 = (bf16[4,128,128]{2,1,0:T(8,128)(2,1)S(1)}, bf16[4,128,128]{2,1,0:T(8,128)(2,1)S(1)}, u32[]{:S(2)}, u32[]{:S(2)}) collective-permute-start(bf16[4,128,128]{2,1,0:T(8,128)(2,1)S(1)} %shard_map.54.refs_3_), channel_id=1, source_target_pairs={{0,4},{1,5},{2,6},{3,7},{4,0},{5,1},{6,2},{7,3},{8,12},{9,13},{10,... | collective-permute-start | bytes 393224 | tf_op jit(solution)/shard_map/ppermute | solution.py:25
  64.7 7.3 %collective-permute-start.4 = (bf16[3,128,128]{2,1,0:T(8,128)(2,1)S(1)}, bf16[3,128,128]{2,1,0:T(8,128)(2,1)S(1)}, u32[]{:S(2)}, u32[]{:S(2)}) collective-permute-start(bf16[3,128,128]{2,1,0:T(8,128)(2,1)S(1)} %shard_map.51), channel_id=1, source_target_pairs={{0,4},{1,5},{2,6},{3,7},{4,0},{5,1},{6,2},{7,3},{8,12},{9,13},{10,... | collective-permute-start | bytes 294920 | tf_op jit(solution)/shard_map/ppermute | solution.py:25
  72.1 21.9 %copy-start.1 = (f32[13,8,512]{2,1,0:T(8,128)S(1)}, f32[13,8,512]{2,1,0:T(8,128)}, u32[]{:S(2)}) copy-start(f32[13,8,512]{2,1,0:T(8,128)} %w_ref.11) | copy-start | bytes 638980
  72.1 30.3 %collective-permute-start.8 = (bf16[28,128,128]{2,1,0:T(8,128)(2,1)S(1)}, bf16[28,128,128]{2,1,0:T(8,128)(2,1)S(1)}, u32[]{:S(2)}, u32[]{:S(2)}) collective-permute-start(bf16[28,128,128]{2,1,0:T(8,128)(2,1)S(1)} %shard_map.55.found_ref), channel_id=1, source_target_pairs={{0,1},{1,0},{2,3},{3,2},{4,5},{5,4},{6,7},{7,6},{8,9},{9,8},{10,11... | collective-permute-start | bytes 2752520 | tf_op jit(solution)/shard_map/ppermute | solution.py:25
  81.5 9.7 %collective-permute-start.9 = (bf16[8,128,128]{2,1,0:T(8,128)(2,1)S(1)}, bf16[8,128,128]{2,1,0:T(8,128)(2,1)S(1)}, u32[]{:S(2)}, u32[]{:S(2)}) collective-permute-start(bf16[8,128,128]{2,1,0:T(8,128)(2,1)S(1)} %pad_maximum_fusion), channel_id=1, source_target_pairs={{0,2},{1,3},{2,0},{3,1},{4,6},{5,7},{6,4},{7,5},{8,10},{9,11},{10,... | collective-permute-start | bytes 786440 | tf_op jit(solution)/shard_map/ppermute | solution.py:25
  91.2 14.3 %collective-permute-start.10 = (bf16[8,128,128]{2,1,0:T(8,128)(2,1)S(1)}, bf16[8,128,128]{2,1,0:T(8,128)(2,1)S(1)}, u32[]{:S(2)}, u32[]{:S(2)}) collective-permute-start(bf16[8,128,128]{2,1,0:T(8,128)(2,1)S(1)} %collective-permute-done.9.found_ref), channel_id=1, source_target_pairs={{0,1},{1,0},{2,3},{3,2},{4,5},{5,4},{6,7},{7,6},{8,9},{9,8},{10,11... | collective-permute-start | bytes 786440 | tf_op jit(solution)/shard_map/ppermute | solution.py:25
  97.3 3.3 %copy-start = (bf16[512,1024]{1,0:T(8,128)(2,1)S(1)}, bf16[512,1024]{1,0:T(8,128)(2,1)}, u32[]{:S(2)}) copy-start(bf16[512,1024]{1,0:T(8,128)(2,1)} %q_ref.7) | copy-start | bytes 3145732

commit v3 on v2

--- a/solution.py
+++ b/solution.py
@@ -62,13 +62,15 @@
     return pl.ds(start if isinstance(start, int) else pl.multiple_of(start, DK), DK)
 
 
-def fetch(pairs, side, sems):
+def fetch(pairs, side, sems, parts=1):
     copies = []
-    for i, (src, dst) in enumerate(pairs):
-        width = dst.shape[1]
-        at = pl.ds(pl.multiple_of(side * width, width), width)
-        copies.append(pltpu.make_async_copy(src.at[:, at], dst, sems.at[i]))
-        copies[-1].start()
+    for part in range(parts):
+        for i, (src, dst) in enumerate(pairs):
+            width = dst.shape[1] // parts
+            at = pl.ds(pl.multiple_of((side * parts + part) * width, width), width)
+            to = dst.at[:, pl.ds(part * width, width)]
+            copies.append(pltpu.make_async_copy(src.at[:, at], to, sems.at[part * len(pairs) + i]))
+            copies[-1].start()
     return copies
 
 
@@ -106,7 +108,7 @@
 
 def local_kernel(other, q_hbm, k_hbm, v_hbm, w_ref, o_ref, q_ref, k_ref, v_ref, sems):
     side = my_place()[1] ^ other
-    copies = fetch(((q_hbm, q_ref), (k_hbm, k_ref), (v_hbm, v_ref)), side, sems)
+    copies = fetch(((q_hbm, q_ref), (k_hbm, k_ref), (v_hbm, v_ref)), side, sems, 2)
     rows = q_ref.shape[0]
     half = o_ref.shape[0]
     tile = 2 * STRETCH
@@ -114,9 +116,10 @@
     tok = lax.broadcasted_iota(jnp.int32, (tile, tile), 1)
     low = jnp.logical_and(tok >= STRETCH, key < STRETCH)
     same = jnp.logical_and(key <= tok, jnp.logical_not(low))
-    for copy in copies:
-        copy.wait()
     for n in range(half):
+        if n % (half // 2) == 0:
+            for copy in copies[3 * (2 * n // half) :][:3]:
+                copy.wait()
         at = lanes(n)
         head = side * half + n
         value_t = v_ref[:, at].T
@@ -148,7 +151,7 @@
         [in_hbm(queries), in_hbm(keys), in_hbm(values), weights],
         flops=2 * rows * rows * width,
         spaces=[HBM, HBM, HBM, VMEM],
-        scratch_shapes=[buffer, buffer, buffer, pltpu.SemaphoreType.DMA((3,))],
+        scratch_shapes=[buffer, buffer, buffer, pltpu.SemaphoreType.DMA((6,))],
     )
 
 
@@ -230,17 +233,8 @@
     return total
 
 
-def send_out(o_ref, sems, out_hbm, copies, total, head):
-    i = len(copies)
-    o_ref[i] = total.astype(BF16).T
-    copies.append(pltpu.make_async_copy(o_ref.at[i], out_hbm.at[:, lanes(head)], sems.at[i]))
-    copies[-1].start()
-
-
-def near_kernel(other, mid, late, local_bits, q_ref, a_ref, w_ref, found_ref, *refs):
-    t_ref, out_hbm, o_ref, sems = refs[-4:]
+def near_kernel(other, mid, late, local_bits, q_ref, a_ref, w_ref, found_ref, t_ref, done_ref):
     half = a_ref.shape[0]
-    copies = []
     for slot in range(half):
         n = slot_head(slot)
         head = (my_place()[1] ^ other) * half + n
@@ -253,24 +247,37 @@
         found = jnp.concatenate(found, axis=0)
         total = add_levels(q_ref, w_ref, a_ref[n], head, found, range(bits), local_bits)
         if slot < 2:
-            send_out(o_ref, sems, out_hbm, copies, total, head)
+            done_ref[slot] = total.astype(BF16).T
         else:
             t_ref[slot - 2] = total
-    for copy in copies:
-        copy.wait()
-
-
-def far_kernel(other, mid, late, local_bits, q_ref, t_ref, w_ref, found_ref, before_hbm, out_hbm, o_ref, sems):
+
+
+def add_far(other, mid, late, local_bits, q_ref, t_ref, w_ref, found_ref, out_hbm, o_ref, sems, copies):
     count = t_ref.shape[0]
-    copies = []
     for i in range(count):
         head = (my_place()[1] ^ other) * 2 * count + slot_head(2 + i)
         found = found_ref[pl.ds(i * late, late)].reshape(late * DK, DK)
         bits = range(3 + mid, 3 + mid + late)
         total = add_levels(q_ref, w_ref, t_ref[i], head, found, bits, local_bits)
-        send_out(o_ref, sems, out_hbm, copies, total, head)
+        o_ref[i] = total.astype(BF16).T
+        copies.append(pltpu.make_async_copy(o_ref.at[i], out_hbm.at[:, lanes(head)], sems.at[len(copies)]))
+        copies[-1].start()
     for copy in copies:
         copy.wait()
+
+
+def far_mine_kernel(mid, late, local_bits, q_ref, t_ref, w_ref, found_ref, own_ref, their_ref, out_hbm, o_ref, sems):
+    copies = []
+    for other, ref in enumerate((own_ref, their_ref)):
+        for slot in range(2):
+            head = (my_place()[1] ^ other) * 2 * t_ref.shape[0] + slot_head(slot)
+            copies.append(pltpu.make_async_copy(ref.at[slot], out_hbm.at[:, lanes(head)], sems.at[len(copies)]))
+            copies[-1].start()
+    add_far(0, mid, late, local_bits, q_ref, t_ref, w_ref, found_ref, out_hbm, o_ref, sems, copies)
+
+
+def far_theirs_kernel(mid, late, local_bits, q_ref, t_ref, w_ref, found_ref, before_hbm, out_hbm, o_ref, sems):
+    add_far(1, mid, late, local_bits, q_ref, t_ref, w_ref, found_ref, out_hbm, o_ref, sems, [])
 
 
 def attend(queries, keys, values, level_weights):
@@ -313,38 +320,36 @@
     )
     theirs = swap(mine, "ctx", 1)
     out_type = jax.ShapeDtypeStruct((rows, width), BF16)
-    out_buffers = lambda n: [pltpu.VMEM((n, rows, DK), BF16), pltpu.SemaphoreType.DMA((n,))]
-
-    def near(other, found, before):
+
+    def near(other, found):
         return kernel_call(
             functools.partial(near_kernel, other, mid, late, local_bits),
-            [jax.ShapeDtypeStruct((half - 2, DK, rows), F32), out_type],
-            [queries, locals_[other], level_weights, found, *before],
+            [jax.ShapeDtypeStruct((2, DK, rows), F32), jax.ShapeDtypeStruct((2, rows, DK), BF16)],
+            [queries, locals_[other], level_weights, found],
             limit=24,
             flops=2 * rows * DK * DK * (half * (3 + mid) + 2 * late),
-            spaces=[VMEM] * 4 + [HBM] * len(before),
-            out_specs=[VMEM, HBM],
-            scratch_shapes=out_buffers(2),
-            input_output_aliases={4: 1} if before else {},
         )
 
-    def far(other, total, found, before):
+    def far(kernel, operands, spaces, copies, **more):
         return kernel_call(
-            functools.partial(far_kernel, other, mid, late, local_bits),
+            functools.partial(kernel, mid, late, local_bits),
             out_type,
-            [queries, total, level_weights, found, before],
+            operands,
             flops=4 * rows * DK * DK * late,
-            spaces=[VMEM] * 4 + [HBM],
+            spaces=spaces,
             out_specs=HBM,
-            scratch_shapes=out_buffers(2),
-            input_output_aliases={4: 0},
+            scratch_shapes=[pltpu.VMEM((2, rows, DK), BF16), pltpu.SemaphoreType.DMA((copies,))],
+            **more,
         )
 
-    own_total, out = near(0, mine, [])
-    other_total, out = near(1, theirs, [out])
+    own_total, own_done = near(0, mine)
+    other_total, other_done = near(1, theirs)
     their23 = swap(slot23, "ctx", 1)
-    out = far(0, own_total, slot23, out)
-    return far(1, other_total, their23, out)
+    out = far(far_mine_kernel, [queries, own_total, level_weights, slot23, own_done, other_done], [VMEM] * 6, 6)
+    return far(
+        far_theirs_kernel, [queries, other_total, level_weights, their23, out],
+        [VMEM] * 4 + [HBM], 2, input_output_aliases={4: 0},
+    )
 
 
 def solution(mesh):

time: 107 us -> 106 us (level)
  transfers between devices with their start and end apart: 12 -> 12, of which waited for: 5 -> 5; matrix products, arithmetic and copies ran while one was open for 0% -> 0% of each run, Pallas kernels for 11% -> 10%
where the time goes in v3:
time: 106 us
  starting transfers between devices  49.4 us (47%)
  blocking collectives  21.1 us (20%)
  waiting for transfers between devices  20 us (19%)
  Pallas kernels  14.8 us (14%)
    ppermute x11, starting transfers between devices, swap(): return lax.ppermute(block, axis, [(i, i ^ stride) for i in range(count)])  42.7 us
    all_to_all x1, blocking collectives, attend(): lax.all_to_all(picked, 'ctx', 0, 0, axis_index_groups=members, tiled=True)  21.1 us
    ppermute x11, waiting for transfers between devices, swap(): return lax.ppermute(block, axis, [(i, i ^ stride) for i in range(count)])  20 us
    pallas_call x15, Pallas kernels, kernel_call(): pl.pallas_call(kernel, out_shape=outs, in_specs=spaces or [VMEM] * len(op...  14.8 us
    all_to_all x1, starting transfers between devices, attend(): run_states = lax.all_to_all(spread, 'grp', 0, 0, tiled=True)  6.76 us
  transfers between devices with their start and end apart: 12, of which 5 were waited for; matrix products, arithmetic and copies ran while one was open for 0% of the time, Pallas kernels for 10%

profile of v3, /device:TPU:1, one launch (start us, length us, event | category | flops | bytes accessed | tf_op | source)
XLA Modules:
  0.0 105.7 jit_solution(8658404834893766432)
XLA Ops:
  0.0 1.7 %shard_map.47 = (bf16[4,128,128]{2,1,0:T(8,128)(2,1)S(1)}, bf16[512,512]{1,0:T(8,128)(2,1)S(1)}, bf16[512,512]{1,0:T(8,128)(2,1)S(1)}) custom-call(bf16[512,1024]{1,0:T(8,128)(2,1)} %k_hbm.5, bf16[512,1024]{1,0:T(8,128)(2,1)} %v_hbm.5), custom_call_target="tpu_custom_call" | custom-call | flops 67108864 | bytes 2097152 | tf_op jit(solution)/shard_map/pallas_call | solution.py:49
  1.8 8.7 %collective-permute-start = (bf16[4,128,128]{2,1,0:T(8,128)(2,1)S(1)}, bf16[4,128,128]{2,1,0:T(8,128)(2,1)S(1)}, u32[]{:S(2)}, u32[]{:S(2)}) collective-permute-start(bf16[4,128,128]{2,1,0:T(8,128)(2,1)S(1)} %get-tuple-element.18), channel_id=1, source_target_pairs={{0,1},{1,0},{2,3},{3,2},{4,5},{5,4},{6,7},{7,6},{8,9},{9,8},{10,11... | collective-permute-start | bytes 393224 | tf_op jit(solution)/shard_map/ppermute | solution.py:25
  10.5 0.3 shard_map.48.keep_ref
  10.9 0.6 collective-permute-done.first_ref
  11.5 1.9 %collective-permute-start.1 = (bf16[2,128,128]{2,1,0:T(8,128)(2,1)S(1)}, bf16[2,128,128]{2,1,0:T(8,128)(2,1)S(1)}, u32[]{:S(2)}, u32[]{:S(2)}) collective-permute-start(bf16[2,128,128]{2,1,0:T(8,128)(2,1)S(1)} %get-tuple-element.19), channel_id=1, source_target_pairs={{0,2},{1,3},{2,0},{3,1},{4,6},{5,7},{6,4},{7,5},{8,10},{9,11},{10,... | collective-permute-start | bytes 196616 | tf_op jit(solution)/shard_map/ppermute | solution.py:25
  13.4 3.1 %collective-permute-done.1.one_ref = bf16[2,128,128]{2,1,0:T(8,128)(2,1)S(1)} collective-permute-done((bf16[2,128,128]{2,1,0:T(8,128)(2,1)S(1)}, bf16[2,128,128]{2,1,0:T(8,128)(2,1)S(1)}, u32[]{:S(2)}, u32[]{:S(2)}) %collective-permute-start.1) | collective-permute-done | bytes 65568 | tf_op jit(solution)/shard_map/ppermute | solution.py:25
  16.5 1.9 %collective-permute-start.3 = (bf16[1,128,128]{2,1,0:T(8,128)(2,1)S(1)}, bf16[1,128,128]{2,1,0:T(8,128)(2,1)S(1)}, u32[]{:S(2)}, u32[]{:S(2)}) collective-permute-start(bf16[1,128,128]{2,1,0:T(8,128)(2,1)S(1)} %shard_map.50), channel_id=1, source_target_pairs={{0,4},{1,5},{2,6},{3,7},{4,0},{5,1},{6,2},{7,3},{8,12},{9,13},{10,... | collective-permute-start | bytes 98312 | tf_op jit(solution)/shard_map/ppermute | solution.py:25
  18.5 4.0 %collective-permute-done.3.two_ref = bf16[1,128,128]{2,1,0:T(8,128)(2,1)S(1)} collective-permute-done((bf16[1,128,128]{2,1,0:T(8,128)(2,1)S(1)}, bf16[1,128,128]{2,1,0:T(8,128)(2,1)S(1)}, u32[]{:S(2)}, u32[]{:S(2)}) %collective-permute-start.3) | collective-permute-done | bytes 32800 | tf_op jit(solution)/shard_map/ppermute | solution.py:25
  22.5 21.1 %all_to_all.10.all_ref = bf16[4,128,128]{2,1,0:T(8,128)(2,1)S(1)} all-to-all(bf16[4,128,128]{2,1,0:T(8,128)(2,1)S(1)} %shard_map.52), channel_id=1, replica_groups={{0,8,16,24},{1,9,17,25},{2,10,18,26},{3,11,19,27},{4,12,20,28},{5,13,21..., dimensions={0} | all-to-all | bytes 262144 | tf_op jit(solution)/shard_map/all_to_all | solution.py:304
  43.6 0.9 shard_map.53
  44.4 6.8 %all-to-all-start.1 = ((bf16[16,128,128]{2,1,0:T(8,128)(2,1)}), bf16[16,128,128]{2,1,0:T(8,128)(2,1)S(1)}, u32[]{:S(2)}, u32[]{:S(2)}) async-start(bf16[16,128,128]{2,1,0:T(8,128)(2,1)} %get-tuple-element.22), calls=%async_computation.1 | async-start | bytes 1048576 | tf_op jit(solution)/shard_map/all_to_all | solution.py:307
  51.2 4.3 %collective-permute-start.5 = (bf16[2,128,128]{2,1,0:T(8,128)(2,1)S(1)}, bf16[2,128,128]{2,1,0:T(8,128)(2,1)S(1)}, u32[]{:S(2)}, u32[]{:S(2)}) collective-permute-start(bf16[2,128,128]{2,1,0:T(8,128)(2,1)S(1)} %get-tuple-element.21.refs_0_), channel_id=1, source_target_pairs={{0,4},{1,5},{2,6},{3,7},{4,0},{5,1},{6,2},{7,3},{8,12},{9,13},{10,... | collective-permute-start | bytes 196616 | tf_op jit(solution)/shard_map/ppermute | solution.py:25
  55.6 1.9 %collective-permute-start.2 = (bf16[2,128,128]{2,1,0:T(8,128)(2,1)S(1)}, bf16[2,128,128]{2,1,0:T(8,128)(2,1)S(1)}, u32[]{:S(2)}, u32[]{:S(2)}) collective-permute-start(bf16[2,128,128]{2,1,0:T(8,128)(2,1)S(1)} %get-tuple-element.20), channel_id=1, source_target_pairs={{0,2},{1,3},{2,0},{3,1},{4,6},{5,7},{6,4},{7,5},{8,10},{9,11},{10,... | collective-permute-start | bytes 196616 | tf_op jit(solution)/shard_map/ppermute | solution.py:25
  57.5 0.0 collective-permute-done.5.refs_1_
  57.5 3.4 %collective-permute-start.6 = (bf16[4,128,128]{2,1,0:T(8,128)(2,1)S(1)}, bf16[4,128,128]{2,1,0:T(8,128)(2,1)S(1)}, u32[]{:S(2)}, u32[]{:S(2)}) collective-permute-start(bf16[4,128,128]{2,1,0:T(8,128)(2,1)S(1)} %pad_maximum_fusion.1), channel_id=1, source_target_pairs={{0,2},{1,3},{2,0},{3,1},{4,6},{5,7},{6,4},{7,5},{8,10},{9,11},{10,... | collective-permute-start | bytes 393224 | tf_op jit(solution)/shard_map/ppermute | solution.py:25
  60.9 0.0 all-to-all-done.1.all_ref
  60.9 0.1 shard_map.54.refs_3_
  61.0 3.6 %collective-permute-start.7 = (bf16[4,128,128]{2,1,0:T(8,128)(2,1)S(1)}, bf16[4,128,128]{2,1,0:T(8,128)(2,1)S(1)}, u32[]{:S(2)}, u32[]{:S(2)}) collective-permute-start(bf16[4,128,128]{2,1,0:T(8,128)(2,1)S(1)} %shard_map.54.refs_3_), channel_id=1, source_target_pairs={{0,4},{1,5},{2,6},{3,7},{4,0},{5,1},{6,2},{7,3},{8,12},{9,13},{10,... | collective-permute-start | bytes 393224 | tf_op jit(solution)/shard_map/ppermute | solution.py:25
  64.6 0.0 collective-permute-done.2.other_ref
  64.7 2.6 %collective-permute-start.4 = (bf16[3,128,128]{2,1,0:T(8,128)(2,1)S(1)}, bf16[3,128,128]{2,1,0:T(8,128)(2,1)S(1)}, u32[]{:S(2)}, u32[]{:S(2)}) collective-permute-start(bf16[3,128,128]{2,1,0:T(8,128)(2,1)S(1)} %shard_map.51), channel_id=1, source_target_pairs={{0,4},{1,5},{2,6},{3,7},{4,0},{5,1},{6,2},{7,3},{8,12},{9,13},{10,... | collective-permute-start | bytes 294920 | tf_op jit(solution)/shard_map/ppermute | solution.py:25
  67.2 4.8 %collective-permute-done.4.rest_ref = bf16[3,128,128]{2,1,0:T(8,128)(2,1)S(1)} collective-permute-done((bf16[3,128,128]{2,1,0:T(8,128)(2,1)S(1)}, bf16[3,128,128]{2,1,0:T(8,128)(2,1)S(1)}, u32[]{:S(2)}, u32[]{:S(2)}) %collective-permute-start.4) | collective-permute-done | bytes 98336 | tf_op jit(solution)/shard_map/ppermute | solution.py:25
  72.0 0.0 collective-permute-done.6.refs_2_
  72.0 0.0 collective-permute-done.7.refs_4_
  72.0 0.1 shard_map.55.found_ref
  72.1 0.0 copy-start.1
  72.1 9.3 %collective-permute-start.8 = (bf16[28,128,128]{2,1,0:T(8,128)(2,1)S(1)}, bf16[28,128,128]{2,1,0:T(8,128)(2,1)S(1)}, u32[]{:S(2)}, u32[]{:S(2)}) collective-permute-start(bf16[28,128,128]{2,1,0:T(8,128)(2,1)S(1)} %shard_map.55.found_ref), channel_id=1, source_target_pairs={{0,1},{1,0},{2,3},{3,2},{4,5},{5,4},{6,7},{7,6},{8,9},{9,8},{10,11... | collective-permute-start | bytes 2752520 | tf_op jit(solution)/shard_map/ppermute | solution.py:25
  81.5 2.1 %collective-permute-start.9 = (bf16[8,128,128]{2,1,0:T(8,128)(2,1)S(1)}, bf16[8,128,128]{2,1,0:T(8,128)(2,1)S(1)}, u32[]{:S(2)}, u32[]{:S(2)}) collective-permute-start(bf16[8,128,128]{2,1,0:T(8,128)(2,1)S(1)} %pad_maximum_fusion), channel_id=1, source_target_pairs={{0,2},{1,3},{2,0},{3,1},{4,6},{5,7},{6,4},{7,5},{8,10},{9,11},{10,... | collective-permute-start | bytes 786440 | tf_op jit(solution)/shard_map/ppermute | solution.py:25
  83.6 7.6 %collective-permute-done.9.found_ref = bf16[8,128,128]{2,1,0:T(8,128)(2,1)S(1)} collective-permute-done((bf16[8,128,128]{2,1,0:T(8,128)(2,1)S(1)}, bf16[8,128,128]{2,1,0:T(8,128)(2,1)S(1)}, u32[]{:S(2)}, u32[]{:S(2)}) %collective-permute-start.9) | collective-permute-done | bytes 262176 | tf_op jit(solution)/shard_map/ppermute | solution.py:25
  91.2 2.8 %collective-permute-start.10 = (bf16[8,128,128]{2,1,0:T(8,128)(2,1)S(1)}, bf16[8,128,128]{2,1,0:T(8,128)(2,1)S(1)}, u32[]{:S(2)}, u32[]{:S(2)}) collective-permute-start(bf16[8,128,128]{2,1,0:T(8,128)(2,1)S(1)} %collective-permute-done.9.found_ref), channel_id=1, source_target_pairs={{0,1},{1,0},{2,3},{3,2},{4,5},{5,4},{6,7},{7,6},{8,9},{9,8},{10,11... | collective-permute-start | bytes 786440 | tf_op jit(solution)/shard_map/ppermute | solution.py:25
  94.0 0.0 copy-done.1
  94.0 3.3 %shard_map.57.a_ref = f32[4,128,512]{2,1,0:T(8,128)S(1)} custom-call(bf16[512,1024]{1,0:T(8,128)(2,1)} %q_ref.7, bf16[512,1024]{1,0:T(8,128)(2,1)} %k_hbm.5, bf16[512,1024]{1,0:T(8,128)(2,1)} %v_hbm.5, f32[13,8,512]{2,1,0:T(8,128)S(1)} %copy-done.1), custom_call_target="tpu_custom_call" | custom-call | flops 536870912 | bytes 3358720 | tf_op jit(solution)/shard_map/pallas_call | solution.py:49
  97.4 0.0 copy-start
  97.4 3.4 %shard_map.46.a_ref = f32[4,128,512]{2,1,0:T(8,128)S(1)} custom-call(bf16[512,1024]{1,0:T(8,128)(2,1)} %q_ref.7, bf16[512,1024]{1,0:T(8,128)(2,1)} %k_hbm.5, bf16[512,1024]{1,0:T(8,128)(2,1)} %v_hbm.5, f32[13,8,512]{2,1,0:T(8,128)S(1)} %copy-done.1), custom_call_target="tpu_custom_call" | custom-call | flops 536870912 | bytes 3358720 | tf_op jit(solution)/shard_map/pallas_call | solution.py:49
  100.8 0.0 copy-done
  100.8 1.1 %shard_map.58 = (f32[2,128,512]{2,1,0:T(8,128)S(1)}, bf16[2,512,128]{2,1,0:T(8,128)(2,1)S(1)}) custom-call(bf16[512,1024]{1,0:T(8,128)(2,1)S(1)} %copy-done, f32[4,128,512]{2,1,0:T(8,128)S(1)} %shard_map.57.a_ref, f32[13,8,512]{2,1,0:T(8,128)S(1)} %copy-done.1, bf16[28,128,128]{2,1,0:T(8,128)(2,1)S(1)} %shard_map.55.found_ref), custom_call_target="tpu_custom_call" | custom-call | flops 469762048 | bytes 3227648 | tf_op jit(solution)/shard_map/pallas_call | solution.py:49
  101.9 0.0 collective-permute-done.8.found_ref
  102.0 1.1 %shard_map.56 = (f32[2,128,512]{2,1,0:T(8,128)S(1)}, bf16[2,512,128]{2,1,0:T(8,128)(2,1)S(1)}) custom-call(bf16[512,1024]{1,0:T(8,128)(2,1)S(1)} %copy-done, f32[4,128,512]{2,1,0:T(8,128)S(1)} %shard_map.46.a_ref, f32[13,8,512]{2,1,0:T(8,128)S(1)} %copy-done.1, bf16[28,128,128]{2,1,0:T(8,128)(2,1)S(1)} %collective-permute-done.8.found_ref), custom_call_target="tpu_custom_call" | custom-call | flops 469762048 | bytes 3227648 | tf_op jit(solution)/shard_map/pallas_call | solution.py:49
  103.1 1.3 %shard_map.59.before_hbm = bf16[512,1024]{1,0:T(8,128)(2,1)} custom-call(bf16[512,1024]{1,0:T(8,128)(2,1)S(1)} %copy-done, f32[2,128,512]{2,1,0:T(8,128)S(1)} %get-tuple-element.24.t_ref, f32[13,8,512]{2,1,0:T(8,128)S(1)} %copy-done.1, bf16[8,128,128]{2,1,0:T(8,128)(2,1)S(1)} %collective-permute-done.9.found_ref, ...), custom_call_target="tpu_custom_call" | custom-call | flops 134217728 | bytes 2572288 | tf_op jit(solution)/shard_map/pallas_call | solution.py:49
  104.4 0.0 collective-permute-done.10.found_ref
  104.4 1.2 %shard_map.60 = bf16[512,1024]{1,0:T(8,128)(2,1)} custom-call(bf16[512,1024]{1,0:T(8,128)(2,1)S(1)} %copy-done, f32[2,128,512]{2,1,0:T(8,128)S(1)} %get-tuple-element.23.t_ref, f32[13,8,512]{2,1,0:T(8,128)S(1)} %copy-done.1, bf16[8,128,128]{2,1,0:T(8,128)(2,1)S(1)} %collective-permute-done.10.found_ref, ...), custom_call_target="tpu_custom_call", output_to_operand_aliasing={{}: (4, {})} | custom-call | flops 134217728 | bytes 3096576 | tf_op jit(solution)/shard_map/pallas_call | solution.py:49
  (6 shorter events, 0.2 us)
Async XLA Ops:
  1.8 9.7 %collective-permute-start = (bf16[4,128,128]{2,1,0:T(8,128)(2,1)S(1)}, bf16[4,128,128]{2,1,0:T(8,128)(2,1)S(1)}, u32[]{:S(2)}, u32[]{:S(2)}) collective-permute-start(bf16[4,128,128]{2,1,0:T(8,128)(2,1)S(1)} %get-tuple-element.18), channel_id=1, source_target_pairs={{0,1},{1,0},{2,3},{3,2},{4,5},{5,4},{6,7},{7,6},{8,9},{9,8},{10,11... | collective-permute-start | bytes 393224 | tf_op jit(solution)/shard_map/ppermute | solution.py:25
  11.5 5.0 %collective-permute-start.1 = (bf16[2,128,128]{2,1,0:T(8,128)(2,1)S(1)}, bf16[2,128,128]{2,1,0:T(8,128)(2,1)S(1)}, u32[]{:S(2)}, u32[]{:S(2)}) collective-permute-start(bf16[2,128,128]{2,1,0:T(8,128)(2,1)S(1)} %get-tuple-element.19), channel_id=1, source_target_pairs={{0,2},{1,3},{2,0},{3,1},{4,6},{5,7},{6,4},{7,5},{8,10},{9,11},{10,... | collective-permute-start | bytes 196616 | tf_op jit(solution)/shard_map/ppermute | solution.py:25
  16.5 5.9 %collective-permute-start.3 = (bf16[1,128,128]{2,1,0:T(8,128)(2,1)S(1)}, bf16[1,128,128]{2,1,0:T(8,128)(2,1)S(1)}, u32[]{:S(2)}, u32[]{:S(2)}) collective-permute-start(bf16[1,128,128]{2,1,0:T(8,128)(2,1)S(1)} %shard_map.50), channel_id=1, source_target_pairs={{0,4},{1,5},{2,6},{3,7},{4,0},{5,1},{6,2},{7,3},{8,12},{9,13},{10,... | collective-permute-start | bytes 98312 | tf_op jit(solution)/shard_map/ppermute | solution.py:25
  44.4 16.5 %all-to-all-start.1 = ((bf16[16,128,128]{2,1,0:T(8,128)(2,1)}), bf16[16,128,128]{2,1,0:T(8,128)(2,1)S(1)}, u32[]{:S(2)}, u32[]{:S(2)}) async-start(bf16[16,128,128]{2,1,0:T(8,128)(2,1)} %get-tuple-element.22), calls=%async_computation.1 | async-start | bytes 1048576 | tf_op jit(solution)/shard_map/all_to_all | solution.py:307
  51.2 6.3 %collective-permute-start.5 = (bf16[2,128,128]{2,1,0:T(8,128)(2,1)S(1)}, bf16[2,128,128]{2,1,0:T(8,128)(2,1)S(1)}, u32[]{:S(2)}, u32[]{:S(2)}) collective-permute-start(bf16[2,128,128]{2,1,0:T(8,128)(2,1)S(1)} %get-tuple-element.21.refs_0_), channel_id=1, source_target_pairs={{0,4},{1,5},{2,6},{3,7},{4,0},{5,1},{6,2},{7,3},{8,12},{9,13},{10,... | collective-permute-start | bytes 196616 | tf_op jit(solution)/shard_map/ppermute | solution.py:25
  55.6 9.1 %collective-permute-start.2 = (bf16[2,128,128]{2,1,0:T(8,128)(2,1)S(1)}, bf16[2,128,128]{2,1,0:T(8,128)(2,1)S(1)}, u32[]{:S(2)}, u32[]{:S(2)}) collective-permute-start(bf16[2,128,128]{2,1,0:T(8,128)(2,1)S(1)} %get-tuple-element.20), channel_id=1, source_target_pairs={{0,2},{1,3},{2,0},{3,1},{4,6},{5,7},{6,4},{7,5},{8,10},{9,11},{10,... | collective-permute-start | bytes 196616 | tf_op jit(solution)/shard_map/ppermute | solution.py:25
  57.5 14.5 %collective-permute-start.6 = (bf16[4,128,128]{2,1,0:T(8,128)(2,1)S(1)}, bf16[4,128,128]{2,1,0:T(8,128)(2,1)S(1)}, u32[]{:S(2)}, u32[]{:S(2)}) collective-permute-start(bf16[4,128,128]{2,1,0:T(8,128)(2,1)S(1)} %pad_maximum_fusion.1), channel_id=1, source_target_pairs={{0,2},{1,3},{2,0},{3,1},{4,6},{5,7},{6,4},{7,5},{8,10},{9,11},{10,... | collective-permute-start | bytes 393224 | tf_op jit(solution)/shard_map/ppermute | solution.py:25
  61.0 11.0 %collective-permute-start.7 = (bf16[4,128,128]{2,1,0:T(8,128)(2,1)S(1)}, bf16[4,128,128]{2,1,0:T(8,128)(2,1)S(1)}, u32[]{:S(2)}, u32[]{:S(2)}) collective-permute-start(bf16[4,128,128]{2,1,0:T(8,128)(2,1)S(1)} %shard_map.54.refs_3_), channel_id=1, source_target_pairs={{0,4},{1,5},{2,6},{3,7},{4,0},{5,1},{6,2},{7,3},{8,12},{9,13},{10,... | collective-permute-start | bytes 393224 | tf_op jit(solution)/shard_map/ppermute | solution.py:25
  64.7 7.3 %collective-permute-start.4 = (bf16[3,128,128]{2,1,0:T(8,128)(2,1)S(1)}, bf16[3,128,128]{2,1,0:T(8,128)(2,1)S(1)}, u32[]{:S(2)}, u32[]{:S(2)}) collective-permute-start(bf16[3,128,128]{2,1,0:T(8,128)(2,1)S(1)} %shard_map.51), channel_id=1, source_target_pairs={{0,4},{1,5},{2,6},{3,7},{4,0},{5,1},{6,2},{7,3},{8,12},{9,13},{10,... | collective-permute-start | bytes 294920 | tf_op jit(solution)/shard_map/ppermute | solution.py:25
  72.1 21.9 %copy-start.1 = (f32[13,8,512]{2,1,0:T(8,128)S(1)}, f32[13,8,512]{2,1,0:T(8,128)}, u32[]{:S(2)}) copy-start(f32[13,8,512]{2,1,0:T(8,128)} %w_ref.11) | copy-start | bytes 638980
  72.1 29.8 %collective-permute-start.8 = (bf16[28,128,128]{2,1,0:T(8,128)(2,1)S(1)}, bf16[28,128,128]{2,1,0:T(8,128)(2,1)S(1)}, u32[]{:S(2)}, u32[]{:S(2)}) collective-permute-start(bf16[28,128,128]{2,1,0:T(8,128)(2,1)S(1)} %shard_map.55.found_ref), channel_id=1, source_target_pairs={{0,1},{1,0},{2,3},{3,2},{4,5},{5,4},{6,7},{7,6},{8,9},{9,8},{10,11... | collective-permute-start | bytes 2752520 | tf_op jit(solution)/shard_map/ppermute | solution.py:25
  81.5 9.7 %collective-permute-start.9 = (bf16[8,128,128]{2,1,0:T(8,128)(2,1)S(1)}, bf16[8,128,128]{2,1,0:T(8,128)(2,1)S(1)}, u32[]{:S(2)}, u32[]{:S(2)}) collective-permute-start(bf16[8,128,128]{2,1,0:T(8,128)(2,1)S(1)} %pad_maximum_fusion), channel_id=1, source_target_pairs={{0,2},{1,3},{2,0},{3,1},{4,6},{5,7},{6,4},{7,5},{8,10},{9,11},{10,... | collective-permute-start | bytes 786440 | tf_op jit(solution)/shard_map/ppermute | solution.py:25
  91.2 13.2 %collective-permute-start.10 = (bf16[8,128,128]{2,1,0:T(8,128)(2,1)S(1)}, bf16[8,128,128]{2,1,0:T(8,128)(2,1)S(1)}, u32[]{:S(2)}, u32[]{:S(2)}) collective-permute-start(bf16[8,128,128]{2,1,0:T(8,128)(2,1)S(1)} %collective-permute-done.9.found_ref), channel_id=1, source_target_pairs={{0,1},{1,0},{2,3},{3,2},{4,5},{5,4},{6,7},{7,6},{8,9},{9,8},{10,11... | collective-permute-start | bytes 786440 | tf_op jit(solution)/shard_map/ppermute | solution.py:25
  97.4 3.4 %copy-start = (bf16[512,1024]{1,0:T(8,128)(2,1)S(1)}, bf16[512,1024]{1,0:T(8,128)(2,1)}, u32[]{:S(2)}) copy-start(bf16[512,1024]{1,0:T(8,128)(2,1)} %q_ref.7) | copy-start | bytes 3145732
